TPU v7x, 256 devices: a whole 4x4x8 slice. The times are simulated.
256 devices in a mesh: dp: 32 (over z, y), expert: 8 (over x, core).
Axes of the slice: x: 4, y: 4, z: 8, core: 2. Of those that a mesh axis runs over, the one named last changes fastest.
Arguments:
- tokens: bfloat16 [8192, 2048], P('dp'), may hold values from -6 to 6
- expert_ids: int32 [8192, 8], P('dp', 'expert'), may hold values from 0 to 127, as said below
- gates: float32 [8192, 8], P('dp', 'expert'), may hold values from 0.05 to 0.25
- positives: int32 [128], P('dp'), may hold values from 0 to 127, as said below
- gate_up: bfloat16 [256, 2048, 768], P(('dp', 'expert')), may hold values from -0.125 to 0.125
- down: bfloat16 [256, 384, 2048], P(('dp', 'expert')), may hold values from -0.21875 to 0.21875
Outputs:
- layer_out: bfloat16 [8192, 2048], P('dp')
- grad_gate_up: bfloat16 [256, 2048, 768], P(('dp', 'expert'))
- grad_down: bfloat16 [256, 384, 2048], P(('dp', 'expert'))
Inputs may be any that keep to these rules, and one draw needn't show every extreme that they name: `expert_ids`: each row names 8 different experts. In the 256 rows of one index of dp no expert is named more than 4 times in one column, and in each column one expert is named exactly 4 times in the rows of every index of dp. positives[i] != i and positives[positives[i]] = i.
All inputs are finite; a program needn't handle non-finite values.
Results may differ from a plain program's by a relative error of at most 0.015.
Values may be sent and summed in bfloat16 or wider, within the bound.
A program may use at most 128 MiB of HBM per device.

v0:
```python
import jax
import jax.numpy as jnp
from jax import lax
from jax.sharding import PartitionSpec as P

logit_divisor = 0.05
grad_scale = 256.0
epsilon = 1e-06


def dispatch(outgoing):
    doubled = jnp.repeat(outgoing, 2, axis=1)
    arrived = lax.all_to_all(
        lax.all_to_all(doubled, "dp", split_axis=0, concat_axis=0, tiled=True),
        "expert",
        split_axis=1,
        concat_axis=1,
        tiled=True,
    )
    return arrived


def contract_rows(left_side, right_side):
    return lax.dot_general(
        left_side, right_side, (((0,), (0,)), ((), ())), preferred_element_type=jnp.float32
    )


def body(tokens, expert_ids, gates, positives, gate_up, down):
    dp_count = lax.axis_size("dp")
    expert_count = lax.axis_size("expert")
    experts = dp_count * expert_count // 2
    owners = expert_count // 2
    tok_dev, model_width = tokens.shape
    routes = expert_ids.shape[1]
    capacity = 2 * tok_dev // experts
    half_width = down.shape[1]
    seq_dev = positives.shape[0]
    seq_length = tok_dev // seq_dev
    lane_rows = routes * capacity
    slot_count = experts * lane_rows
    labels = jnp.arange(experts, dtype=jnp.int32)
    onehot = (expert_ids[:, :, None] == labels).astype(jnp.int32)
    before = jnp.cumsum(onehot, axis=0) - onehot
    position = jnp.sum(before * onehot, axis=2)
    column = jnp.arange(routes, dtype=jnp.int32)[None, :]
    slot_of = (expert_ids * routes + column) * capacity + position
    spread = tokens[:, None, :].reshape(tok_dev * routes, model_width)
    outgoing = (
        jnp.zeros((slot_count, model_width), jnp.bfloat16).at[slot_of.reshape(-1)].set(spread)
    )
    arrived = dispatch(outgoing.reshape(dp_count, owners, lane_rows, model_width))
    expert_rows = arrived.reshape(-1, model_width)
    weight_in = gate_up[0]
    weight_out = down[0]
    projected = jnp.dot(expert_rows, weight_in, preferred_element_type=jnp.float32)
    gate_part = projected[:, :half_width]
    up_part = projected[:, half_width:]
    sigmoid_gate = jax.nn.sigmoid(gate_part)
    activated = gate_part * sigmoid_gate
    hidden = (activated * up_part).astype(jnp.bfloat16)
    half_out = jnp.dot(hidden, weight_out, preferred_element_type=jnp.float32).astype(jnp.bfloat16)
    returned = lax.all_to_all(
        lax.all_to_all(
            half_out.reshape(dp_count, expert_count, lane_rows, model_width),
            "dp",
            split_axis=0,
            concat_axis=0,
            tiled=True,
        ),
        "expert",
        split_axis=1,
        concat_axis=1,
        tiled=True,
    )
    paired = returned.reshape(dp_count, owners, 2, lane_rows, model_width)
    route_out = (paired[:, :, 0].astype(jnp.float32) + paired[:, :, 1].astype(jnp.float32)).reshape(
        slot_count, model_width
    )
    picked = route_out[slot_of.reshape(-1)].reshape(tok_dev, routes, model_width)
    contrib = jnp.sum(gates[:, :, None] * picked, axis=1)
    summed = lax.psum(contrib.astype(jnp.bfloat16), "expert").astype(jnp.float32)
    layer_out = (tokens.astype(jnp.float32) + summed).astype(jnp.bfloat16)
    last_rows = layer_out[seq_length - 1 :: seq_length]
    gathered = lax.all_gather(last_rows, "dp", axis=0, tiled=True)
    gathered_values = gathered.astype(jnp.float32)
    norms_every_row = jnp.sqrt(jnp.sum(gathered_values * gathered_values, axis=1) + epsilon)
    last_values = last_rows.astype(jnp.float32)
    norms_local_rows = jnp.sqrt(jnp.sum(last_values * last_values, axis=1) + epsilon)
    row_start = lax.axis_index("dp") * seq_dev
    columns_all = jnp.arange(gathered.shape[0], dtype=jnp.int32)
    own_index = row_start + jnp.arange(seq_dev, dtype=jnp.int32)
    target = (columns_all[None, :] == positives[:, None]).astype(jnp.float32)
    unit_all = gathered_values / norms_every_row[:, None]
    unit_own = last_values / norms_local_rows[:, None]
    pairwise_dots = lax.dot_general(
        last_rows, gathered, (((1,), (1,)), ((), ())), preferred_element_type=jnp.float32
    )
    cosine_logits = (
        pairwise_dots / (norms_local_rows[:, None] * norms_every_row[None, :]) / logit_divisor
    )
    keep_mask = columns_all[None, :] != own_index[:, None]
    exp_scores = jnp.where(keep_mask, jnp.exp(cosine_logits), 0.0)
    probabilities = exp_scores / jnp.sum(exp_scores, axis=1, keepdims=True)
    objective_multiplier = grad_scale * (probabilities - target)
    forward_terms = (
        jnp.dot(
            objective_multiplier,
            unit_all,
            precision=lax.Precision.HIGHEST,
            preferred_element_type=jnp.float32,
        )
        / logit_divisor
    )
    reverse_local = (
        lax.dot_general(
            objective_multiplier,
            unit_own,
            (((0,), (0,)), ((), ())),
            precision=lax.Precision.HIGHEST,
            preferred_element_type=jnp.float32,
        )
        / logit_divisor
    )
    reverse_own = lax.psum_scatter(
        reverse_local.astype(jnp.bfloat16), "dp", scatter_dimension=0, tiled=True
    ).astype(jnp.float32)
    slope_wrt_unit_embedding = forward_terms + reverse_own
    projection = jnp.sum(unit_own * slope_wrt_unit_embedding, axis=1, keepdims=True)
    grad_last = (slope_wrt_unit_embedding - unit_own * projection) / norms_local_rows[:, None]
    slot_last = slot_of[seq_length - 1 :: seq_length]
    gates_last = gates[seq_length - 1 :: seq_length]
    route_grad = (gates_last[:, :, None] * grad_last[:, None, :]).astype(jnp.bfloat16)
    backward_out = (
        jnp.zeros((slot_count, model_width), jnp.bfloat16)
        .at[slot_last.reshape(-1)]
        .set(route_grad.reshape(-1, model_width))
    )
    grad_rows = dispatch(backward_out.reshape(dp_count, owners, lane_rows, model_width)).reshape(
        -1, model_width
    )
    grad_hidden = lax.dot_general(
        grad_rows, weight_out, (((1,), (1,)), ((), ())), preferred_element_type=jnp.float32
    )
    grad_down = contract_rows(hidden, grad_rows).astype(jnp.bfloat16)
    gate_slope = sigmoid_gate * (1.0 + gate_part * (1.0 - sigmoid_gate))
    grad_projected = jnp.concatenate(
        [grad_hidden * up_part * gate_slope, grad_hidden * activated], axis=1
    ).astype(jnp.bfloat16)
    grad_gate_up = contract_rows(expert_rows, grad_projected).astype(jnp.bfloat16)
    return (layer_out, grad_gate_up[None], grad_down[None])


def solution(mesh):
    return jax.shard_map(
        body,
        mesh=mesh,
        in_specs=(
            P("dp", None),
            P("dp", "expert"),
            P("dp", "expert"),
            P("dp"),
            P(("dp", "expert"), None, None),
            P(("dp", "expert"), None, None),
        ),
        out_specs=(P("dp", None), P(("dp", "expert"), None, None), P(("dp", "expert"), None, None)),
        check_vma=False,
    )
```

profile of v0, /device:TPU:1, one launch (start us, length us, event | category | flops | bytes accessed | tf_op | source)
XLA Modules:
  0.0 850.0 jit_solution(14433231337294980714)
XLA Ops:
  7.2 0.0 copy-start
  7.2 0.9 fusion.26
  8.1 0.1 fusion.24
  8.3 0.9 fusion.23
  9.2 0.7 compare_select_fusion
  9.9 4.4 scatter_custom_fusion
  14.3 4.1 reshape.188
  18.4 3.7 broadcast_in_dim.11
  22.1 105.4 %all_to_all.30 = bf16[32,8,4,2048]{3,2,1,0:T(4,128)(2,1)S(1)} all-to-all(bf16[32,8,4,2048]{3,2,1,0:T(4,128)(2,1)S(1)} %bitcast.57), channel_id=1, replica_groups=mesh['dp'=32,'expert'=8] {'dp'}, dimensions={0} | all-to-all | bytes 8388608 | tf_op jit(solution)/shard_map/all_to_all | solution.py:14
  127.5 2.1 copy.33
  129.6 55.7 %all_to_all.31 = bf16[32,8,4,2048]{3,2,0,1:T(4,128)(2,1)S(1)} all-to-all(bf16[32,8,4,2048]{3,2,0,1:T(4,128)(2,1)S(1)} %copy.33), channel_id=1, replica_groups=mesh['dp'=32,'expert'=8] {'expert'}, dimensions={1} | all-to-all | bytes 8388608 | tf_op jit(solution)/shard_map/all_to_all | solution.py:13
  185.3 4.0 copy.34
  189.4 6.9 reshape.190
  196.3 5.3 fusion
  201.6 0.0 copy-start.4
  201.6 1.7 copy-done.4
  203.3 0.5 multiply_convert_fusion.3
  203.8 0.9 copy-done.11
  204.7 4.4 convolution_convert_fusion
  209.0 7.2 reshape.191
  216.2 98.7 %all_to_all.32 = bf16[32,8,4,2048]{3,2,1,0:T(4,128)(2,1)S(1)} all-to-all(bf16[32,8,4,2048]{3,2,1,0:T(4,128)(2,1)} %reshape.191), channel_id=1, replica_groups=mesh['dp'=32,'expert'=8] {'dp'}, dimensions={0} | all-to-all | bytes 8388608 | tf_op jit(solution)/shard_map/all_to_all | solution.py:64
  314.9 4.1 copy.35
  319.0 7.4 all-to-all-start.3
  326.4 0.2 all-reduce.4.cloned.1.call-start
  326.7 48.6 %all-to-all-done.3 = bf16[32,8,4,2048]{3,2,0,1:T(4,128)(2,1)} async-done(((bf16[32,8,4,2048]{3,2,0,1:T(4,128)(2,1)}), bf16[32,8,4,2048]{3,2,0,1:T(4,128)(2,1)}, u32[]{:S(2)}, u32[]{:S(2)}) %all-to-all-start.3) | async-done | bytes 4194336 | tf_op jit(solution)/shard_map/all_to_all | solution.py:63
  375.2 3.5 fusion.36
  378.7 3.9 convert_add_fusion
  382.6 5.3 add.70
  387.9 4.6 gather_fusion
  392.5 0.0 copy-done.10
  392.6 0.0 copy-start.7
  392.6 1.1 multiply_convert_fusion
  393.7 0.0 all-reduce.4.cloned.1.call-update
  393.7 0.0 all-reduce.6.cloned.1.call-start
  393.8 61.3 %all-reduce.4.cloned.1.call-done = bf16[256,2048]{1,0:T(8,128)(2,1)} async-done(((bf16[256,2048]{1,0:T(8,128)(2,1)}), bf16[256,2048]{1,0:T(8,128)(2,1)}) %all-reduce.4.cloned.1.call-update) | async-done | bytes 1048592 | tf_op jit(solution)/shard_map/psum | solution.py:82
  455.1 1.6 add_convert_fusion
  456.8 0.0 copy-start.6
  456.8 0.0 copy-start.12
  456.8 0.0 copy-start.13
  456.8 0.1 slice.35
  456.9 0.1 fusion.27
  457.0 0.7 copy-done.6
  457.7 39.1 %all-gather = bf16[32,4,2048]{2,1,0:T(4,128)(2,1)S(1)} all-gather(bf16[1,4,2048]{2,1,0:T(4,128)(2,1)S(1)} %bitcast.62), channel_id=1, replica_groups=mesh['dp'=32,'expert'=8] {'dp'}, dimensions={0}, use_global_device_ids=true | all-gather | bytes 540672 | tf_op jit(solution)/shard_map/all_gather | solution.py:85
  496.8 0.1 reshape.221
  496.9 0.2 fusion.16
  497.1 0.4 fusion.37
  497.5 1.9 fusion.4
  499.4 0.0 all-reduce.6.cloned.1.call-update
  499.5 0.1 slice.34
  499.6 0.1 slice.33
  499.7 0.6 dynamic-slice
  500.9 152.2 %all-reduce.6.cloned.1.call-done = bf16[128,2048]{1,0:T(8,128)(2,1)} async-done(((bf16[128,2048]{1,0:T(8,128)(2,1)}), bf16[128,2048]{1,0:T(8,128)(2,1)}) %all-reduce.6.cloned.1.call-update) | async-done | bytes 524304
  653.1 1.6 multiply_reduce_fusion
  654.7 2.5 scatter_custom_fusion.1
  657.2 2.7 reshape.193
  659.9 2.1 broadcast_in_dim.13
  662.1 94.5 %all_to_all.33 = bf16[32,8,4,2048]{3,2,1,0:T(4,128)(2,1)S(1)} all-to-all(bf16[32,8,4,2048]{3,2,1,0:T(4,128)(2,1)S(1)} %bitcast.58), channel_id=1, replica_groups=mesh['dp'=32,'expert'=8] {'dp'}, dimensions={0} | all-to-all | bytes 8388608 | tf_op jit(solution)/shard_map/all_to_all | solution.py:14
  756.6 2.1 copy.38
  758.7 59.9 %all_to_all.34 = bf16[32,8,4,2048]{3,2,0,1:T(4,128)(2,1)S(1)} all-to-all(bf16[32,8,4,2048]{3,2,0,1:T(4,128)(2,1)S(1)} %copy.38), channel_id=1, replica_groups=mesh['dp'=32,'expert'=8] {'expert'}, dimensions={1} | all-to-all | bytes 8388608 | tf_op jit(solution)/shard_map/all_to_all | solution.py:13
  818.6 4.0 copy.39
  822.6 7.1 reshape.195
  829.7 5.1 multiply_convert_fusion.2
  834.8 3.0 fusion.3
  837.8 4.9 fusion.2
  (28 shorter events, 0.1 us)
Async XLA Ops:
  7.2 189.1 %copy-start = (bf16[1,2048,768]{2,1,0:T(8,128)(2,1)S(1)}, bf16[1,2048,768]{2,1,0:T(8,128)(2,1)}, u32[]{:S(2)}) copy-start(bf16[1,2048,768]{2,1,0:T(8,128)(2,1)} %param.10) | copy-start | bytes 9437188
  201.6 1.7 copy-start.4
  203.3 1.4 copy-start.11
  204.7 4.4 copy-start.8
  319.0 56.3 %all-to-all-start.3 = ((bf16[32,8,4,2048]{3,2,0,1:T(4,128)(2,1)}), bf16[32,8,4,2048]{3,2,0,1:T(4,128)(2,1)}, u32[]{:S(2)}, u32[]{:S(2)}) async-start(bf16[32,8,4,2048]{3,2,0,1:T(4,128)(2,1)} %copy.35), calls=%async_computation.3 | async-start | bytes 8388608 | tf_op jit(solution)/shard_map/all_to_all | solution.py:63
  326.4 128.7 %all-reduce.4.cloned.1.call-start = ((), (), s32[]{:S(2)}) async-start(), calls=%async_computation.6 | async-start | bytes 2097152 | tf_op jit(solution)/shard_map/psum | solution.py:82
  387.9 4.6 copy-start.10
  392.6 62.6 %copy-start.7 = (bf16[256,2048]{1,0:T(8,128)(2,1)S(1)}, bf16[256,2048]{1,0:T(8,128)(2,1)}, u32[]{:S(2)}) copy-start(bf16[256,2048]{1,0:T(8,128)(2,1)} %param.6) | copy-start | bytes 3145732
  393.7 259.4 %all-reduce.6.cloned.1.call-start = ((), (), s32[]{:S(2)}) async-start(), calls=%async_computation.7 | async-start | bytes 1048576
  456.8 1.0 copy-start.6
  456.8 40.7 %copy-start.12 = (s32[4]{0:T(128)S(1)}, s32[4]{0:T(128)}, u32[]{:S(2)}) copy-start(s32[4]{0:T(128)} %param.9) | copy-start | bytes 52
  456.8 42.9 %copy-start.13 = (u32[256]{0:T(256)S(1)}, u32[256]{0:T(256)}, u32[]{:S(2)}) copy-start(u32[256]{0:T(256)} %constant.45) | copy-start | bytes 3076
  822.6 7.1 copy-start.5
  829.7 5.1 copy-start.3
  829.7 5.1 copy-start.9
  834.8 3.0 copy-start.2
  837.8 4.9 copy-start.1
Sparse Core Ops, SparseCore 0:
  393.9 61.2 all-reduce.3
  499.6 153.4 all-reduce.5
where the time goes:
time: 857 us; the launch traced here: 850 us
  blocking collectives  453 us (53%)
  waiting for transfers between devices  262 us (31%)
  local copies, waits for them, and re-layouts  72.3 us (8%)
  matrix products  26.5 us (3%)
  between operations  15.4 us (2%)
  other arithmetic  12.6 us (1%)
    all_to_all x2, blocking collectives, dispatch(): lax.all_to_all(doubled, 'dp', split_axis=0, concat_axis=0, tiled=True)  200 us
    unnamed x3, waiting for transfers between devices  152 us
    all_to_all x2, blocking collectives, dispatch(): lax.all_to_all(lax.all_to_all(doubled, 'dp', split_axis=0, concat_axis=0,...  116 us
    all_to_all x1, blocking collectives, body(): lax.all_to_all(half_out.reshape(dp_count, expert_count, lane_rows, model_...  98.7 us
    psum x1, waiting for transfers between devices, body(): lax.psum(contrib.astype(jnp.bfloat16), 'expert').astype(jnp.float32)  61.3 us
    all_to_all x1, waiting for transfers between devices, body(): lax.all_to_all(lax.all_to_all(half_out.reshape(dp_count, expert_count, la...  48.6 us
    all_gather x1, blocking collectives, body(): gathered = lax.all_gather(last_rows, 'dp', axis=0, tiled=True)  39.1 us
  transfers between devices with their start and end apart: 3, of which 3 were waited for; matrix products, arithmetic and copies ran while one was open for 0% of the time, Pallas kernels for 0%

commit v1 on v0

v1 whole, which is shorter than its diff:
```python
import functools

import jax
import jax.numpy as jnp
from jax import lax
from jax.experimental import pallas as pl
from jax.experimental.pallas import tpu as pltpu
from jax.sharding import PartitionSpec as P

logit_divisor = 0.05
grad_scale = 256.0
epsilon = 1e-06

MESH = pl.DeviceIdType.MESH
NZ, NY, NX, NC = 8, 4, 4, 2
NQ = NY * NX
SLOTS = 32


def layer_kernel(
    tok_hbm, meta_ref, gu_hbm, dn_hbm,
    out_hbm, last_ref, xlast_ref, ml_ref,
    zbuf, mb, mt, rk, gw, tri, sbuf, xm, gu, dn, hid, ys, yo, yr, rs, rbuf, pacc, prec, psend,
    outb, ly, lz, lx, xly, xlz, xlx, mly,
    loc_sem, own_sem, mb_send, mb_recv, mc_send, mc_recv, zs_sem, zr_sem, ms_sem, mr_sem,
    xs_sem, xr_sem, xf_send, xf_recv, ys_send, ys_recv, rs_sem, rr_sem, rown_sem, ps_sem, pr_sem,
    ob_send, ob_recv, oc_send, oc_recv,
    l_send, l_recv, xl_send, xl_recv, mls_sem, mlr_sem,
):
    dp = lax.axis_index("dp")
    ex = lax.axis_index("expert")
    z, y, x, c = dp // NY, dp % NY, ex // NC, ex % NC
    q_me = y * NX + x
    tok, ds = zbuf.shape[1], zbuf.shape[2]
    rows = NY * SLOTS
    core = (dp, x * NC + (1 - c))

    def at(zz, yy, xx):
        return (zz * NY + yy, xx * NC + c)

    def z_line(r):
        return at((z + r) % NZ, y, x)

    def y_line(r):
        return at(z, (y + r) % NY, x)

    def x_line(r):
        return at(z, y, (x + r) % NX)

    def plane(r):
        q = (q_me + r) % NQ
        return q, at(z, q // NX, q % NX)

    def remote(src, dst, send, recv, device):
        return pltpu.make_async_remote_copy(
            src_ref=src, dst_ref=dst, send_sem=send, recv_sem=recv,
            device_id=device, device_id_type=MESH,
        )

    def drain(ref, sem):
        pltpu.make_async_copy(ref, ref, sem).wait()

    col_me = pl.multiple_of(ex * ds, ds)
    tok_load = pltpu.make_async_copy(tok_hbm.at[:, pl.ds(col_me, ds)], zbuf.at[0], loc_sem.at[0])
    tok_load.start()
    half = hid.shape[1]
    nch = gu.shape[0]
    ch = half // nch
    loads = []
    for n in range(nch):
        for part in range(2):
            loads.append(pltpu.make_async_copy(
                gu_hbm.at[:, pl.ds(part * half + n * ch, ch)],
                gu.at[n, :, pl.ds(part * ch, ch)], loc_sem.at[1 + 2 * n + part]))
    for j in range(NX * NC):
        loads.append(pltpu.make_async_copy(
            dn_hbm.at[:, pl.ds(j * ds, ds)], dn.at[j], loc_sem.at[1 + 2 * nch + j]))
    for load in loads:
        load.start()

    barrier = pltpu.get_barrier_semaphore()

    @pl.loop(1, NZ)
    def _(r):
        pl.semaphore_signal(barrier, inc=1, device_id=z_line(r), device_id_type=MESH)

    @pl.loop(1, NQ)
    def _(r):
        pl.semaphore_signal(barrier, inc=1, device_id=plane(r)[1], device_id_type=MESH)

    pl.semaphore_signal(barrier, inc=1, device_id=core, device_id_type=MESH)
    mb[c, x] = meta_ref[...]
    ti = lax.broadcasted_iota(jnp.int32, (tok, tok), 0)
    tj = lax.broadcasted_iota(jnp.int32, (tok, tok), 1)
    tri[...] = jnp.where(ti < tj, 1.0, 0.0).astype(jnp.bfloat16)
    pl.semaphore_wait(barrier, NZ + NQ - 1)

    for r in range(1, NX):
        remote(mb.at[c, x], mb.at[c, x], mb_send.at[r - 1], mb_recv.at[r - 1], x_line(r)).start()

    up, down = z_line(1), z_line(NZ - 1)
    tok_load.wait()
    remote(zbuf.at[0], zbuf.at[1], zs_sem.at[6], zr_sem.at[1], down).start()
    remote(zbuf.at[0], zbuf.at[2], zs_sem.at[0], zr_sem.at[2], up).start()

    per = 4
    length = tok // per
    lrow = lax.broadcasted_iota(jnp.int32, (NY * per, tok), 0)
    ltok = lax.broadcasted_iota(jnp.int32, (NY * per, tok), 1)
    last_sel = jnp.where(
        (ltok % length == length - 1) & (lrow == y * per + ltok // length), 1.0, 0.0
    ).astype(jnp.bfloat16)

    def l_y_start(block, buf, send, recv):
        picked = jnp.dot(last_sel, block, preferred_element_type=jnp.float32)
        buf[y] = picked.astype(jnp.bfloat16)
        for r in range(1, NY):
            remote(buf.at[y], buf.at[y], send.at[r - 1], recv.at[r - 1], y_line(r)).start()

    def l_z_start(ybuf, buf, send, recv):
        for r in range(1, NY):
            drain(ybuf.at[0], recv.at[r - 1])
        total = ybuf[0].astype(jnp.float32)
        for r in range(1, NY):
            total += ybuf[r].astype(jnp.float32)
        buf[z] = total.astype(jnp.bfloat16)
        for r in range(1, NZ):
            remote(buf.at[z], buf.at[z], send.at[2 + r], recv.at[2 + r], z_line(r)).start()

    def l_x_start(zb, buf, send, recv):
        for r in range(1, NZ):
            drain(zb.at[0], recv.at[2 + r])
        buf[c, x] = zb[...].reshape(NZ * NY * per, ds)
        for r in range(1, NX):
            remote(buf.at[c, x], buf.at[c, x], send.at[9 + r], recv.at[9 + r], x_line(r)).start()

    def l_c_start(buf, send, recv):
        for r in range(1, NX):
            drain(buf.at[0, 0], recv.at[9 + r])
        remote(buf.at[c], buf.at[c], send.at[13], recv.at[13], core).start()

    def l_finish(ybuf, zb, buf, out, send, recv):
        drain(buf.at[0], recv.at[13])
        out[...] = buf[...].reshape(out.shape)
        for r in range(1, NY):
            drain(ybuf.at[0], send.at[r - 1])
        for r in range(1, NZ):
            drain(zb.at[0], send.at[2 + r])
        for r in range(1, NX):
            drain(buf.at[0, 0], send.at[9 + r])
        drain(buf.at[0], send.at[13])

    l_y_start(zbuf[0], xly, xl_send, xl_recv)

    for r in range(1, NX):
        drain(mb.at[0, 0], mb_recv.at[r - 1])
    remote(mb.at[c], mb.at[c], mc_send, mc_recv, core).start()
    drain(mb.at[0], mc_recv)
    for part in range(2):
        for side in range(2):
            for cc in range(NC):
                mt[0, part * 8 + cc * NX:part * 8 + (cc + 1) * NX, side * 128:(side + 1) * 128] = (
                    mb[cc, :, 2 * part + side, :])
    for side in range(2):
        mt[0, 16:24, side * 128:(side + 1) * 128] = jnp.broadcast_to(
            mb[0, 0, 4 + side:5 + side, :], (8, 128))
    remote(mt.at[0], mt.at[1], ms_sem.at[6], mr_sem.at[1], down).start()
    remote(mt.at[0], mt.at[2], ms_sem.at[0], mr_sem.at[2], up).start()

    slot_iota = lax.broadcasted_iota(jnp.int32, (SLOTS, tok), 0).astype(jnp.float32)

    def gather_block(i):
        ids = mt[i, 0:8, :]
        gate = mt[i, 8:16, :]
        hits, weights = [], []
        for q in range(NQ):
            hit = ids == (z * NQ + q).astype(jnp.float32)
            hits.append(jnp.sum(jnp.where(hit, 1.0, 0.0), axis=0, keepdims=True))
            weights.append(jnp.sum(jnp.where(hit, gate, 0.0), axis=0, keepdims=True))
        hit = jnp.concatenate(hits, axis=0)
        rank = jnp.dot(hit.astype(jnp.bfloat16), tri[...], preferred_element_type=jnp.float32)
        ranked = jnp.where(hit > 0.0, rank, -1.0)
        rk[i] = ranked
        gw[i] = jnp.concatenate(weights, axis=0)
        picks = jnp.concatenate(
            [jnp.where(slot_iota == ranked[q:q + 1, :], 1.0, 0.0) for q in range(NQ)], axis=0
        ).astype(jnp.bfloat16)
        got = jnp.dot(picks, zbuf[i], preferred_element_type=jnp.float32)
        sbuf[i] = got.astype(jnp.bfloat16).reshape(NQ, SLOTS, ds)

        def place():
            return xm.at[i, pl.ds(pl.multiple_of(y * SLOTS, SLOTS), SLOTS), pl.ds(col_dst, ds)]

        col_dst = pl.multiple_of((x * NC + c) * ds, ds)

        @pl.loop(1, NQ)
        def _(r):
            q, device = plane(r)
            remote(sbuf.at[i, q], place(), xs_sem.at[i], xr_sem.at[i], device).start()

        pltpu.make_async_copy(sbuf.at[i, q_me], place(), own_sem.at[i]).start()

    gather_block(0)

    @pl.loop(1, NZ)
    def _(i):
        drain(zbuf.at[0], zr_sem.at[i])
        drain(mt.at[0], mr_sem.at[i])

        @pl.when(i <= 5)
        def _():
            device = at((z + 1 - 2 * (i % 2) + NZ) % NZ, y, x)
            remote(zbuf.at[i], zbuf.at[i + 2], zs_sem.at[i], zr_sem.at[i + 2], device).start()
            remote(mt.at[i], mt.at[i + 2], ms_sem.at[i], mr_sem.at[i + 2], device).start()

        gather_block(i)

        @pl.when(i == 2)
        def _():
            l_z_start(xly, xlz, xl_send, xl_recv)

        @pl.when(i == 5)
        def _():
            l_x_start(xlz, xlx, xl_send, xl_recv)

    l_c_start(xlx, xl_send, xl_recv)

    total = jnp.zeros((24, NZ * NY * per), jnp.float32)
    st = lax.broadcasted_iota(jnp.int32, (tok, NZ * NY * per), 0)
    sc = lax.broadcasted_iota(jnp.int32, (tok, NZ * NY * per), 1)
    for i in range(NZ):
        zi = (z + ((i + 1) // 2) * (2 * (i % 2) - 1) + NZ) % NZ
        sel = jnp.where(
            (st % length == length - 1) & (sc == (zi * NY + y) * per + st // length), 1.0, 0.0)
        total += jnp.dot(mt[i], sel, precision=lax.Precision.HIGHEST,
                         preferred_element_type=jnp.float32)
    mly[y] = total
    for r in range(1, NY):
        remote(mly.at[y], mly.at[y], mls_sem.at[r - 1], mlr_sem.at[r - 1], y_line(r)).start()

    def forward(i):
        drain(sbuf.at[i, pl.ds(0, NQ - 1)], xr_sem.at[i])
        drain(sbuf.at[0, 0], own_sem.at[i])
        for xx in range(NX):
            cols = pl.ds(pl.multiple_of((xx * NC + c) * ds, ds), ds)
            remote(xm.at[i, :, cols], xm.at[i, :, cols], xf_send.at[i], xf_recv.at[i], core).start()

    for load in loads:
        load.wait()
    forward(0)
    forward(1)

    @pl.loop(0, NZ // 2)
    def _(p):
        @pl.when(p < NZ // 2 - 1)
        def _():
            forward(2 * p + 2)
            forward(2 * p + 3)

        for b in range(2):
            drain(xm.at[0, :, pl.ds(0, NX * ds)], xf_recv.at[2 * p + b])
        xrows = xm[pl.ds(2 * p, 2)].reshape(2 * rows, NX * NC * ds)
        for n in range(nch):
            pr = jnp.dot(xrows, gu[n], preferred_element_type=jnp.float32)
            g, u = pr[:, :ch], pr[:, ch:]
            hid[:, n * ch:(n + 1) * ch] = (g * jax.nn.sigmoid(g) * u).astype(jnp.bfloat16)
        hv = hid[...]
        for xx in range(NX):
            o = jnp.dot(hv, dn[xx * NC + 1 - c], preferred_element_type=jnp.float32)
            o = o.astype(jnp.bfloat16)
            ys[2 * p, xx] = o[:rows]
            ys[2 * p + 1, xx] = o[rows:]
        for b in range(2):
            remote(ys.at[2 * p + b], yr.at[2 * p + b], ys_send.at[2 * p + b],
                   ys_recv.at[2 * p + b], core).start()
        for xx in range(NX):
            o = jnp.dot(hv, dn[xx * NC + c], preferred_element_type=jnp.float32)
            o = o.astype(jnp.bfloat16)
            yo[2 * p, xx] = o[:rows]
            yo[2 * p + 1, xx] = o[rows:]

    @pl.loop(0, NZ)
    def _(n):
        i = NZ - 1 - n
        drain(ys.at[0], ys_recv.at[i])
        rs[i] = (yo[i].astype(jnp.float32) + yr[i].astype(jnp.float32)).astype(jnp.bfloat16)

        def piece(q):
            return rs.at[i, q % NX, pl.ds(pl.multiple_of((q // NX) * SLOTS, SLOTS), SLOTS)]

        @pl.loop(1, NQ)
        def _(r):
            q, device = plane(r)
            remote(piece(q), rbuf.at[i, q_me], rs_sem.at[i], rr_sem.at[i], device).start()

        pltpu.make_async_copy(piece(q_me), rbuf.at[i, q_me], rown_sem.at[i]).start()

    def combine(i):
        drain(sbuf.at[i, pl.ds(0, NQ - 1)], rr_sem.at[i])
        drain(sbuf.at[0, 0], rown_sem.at[i])
        ranked, w = rk[i], gw[i]
        spread = jnp.concatenate(
            [jnp.where(slot_iota == ranked[q:q + 1, :], w[q:q + 1, :], 0.0) for q in range(NQ)],
            axis=0,
        ).astype(jnp.bfloat16)
        return lax.dot_general(
            spread, rbuf[i].reshape(NQ * SLOTS, ds), (((0,), (0,)), ((), ())),
            preferred_element_type=jnp.float32)

    @pl.loop(0, NZ - 1)
    def _(n):
        i = NZ - 1 - n
        part = combine(i)
        pacc[i] = part

        @pl.when(i <= 5)
        def _():
            drain(prec.at[0], pr_sem.at[i])
            pacc[i] += prec[i].astype(jnp.float32)

        prec_out = pacc[i].astype(jnp.bfloat16)
        psend[i] = prec_out
        slot = (i + 5) % 7
        device = at((z - 1 + 2 * (i % 2) + NZ) % NZ, y, x)
        remote(psend.at[i], prec.at[slot], ps_sem.at[i], pr_sem.at[slot], device).start()

    part = combine(0)
    drain(prec.at[0], pr_sem.at[0])
    drain(prec.at[0], pr_sem.at[6])
    part += prec[0].astype(jnp.float32) + prec[6].astype(jnp.float32)
    block = (zbuf[0].astype(jnp.float32) + part).astype(jnp.bfloat16)
    outb[c, x] = block
    l_y_start(block, ly, l_send, l_recv)
    for r in range(1, NX):
        remote(outb.at[c, x], outb.at[c, x], ob_send.at[r - 1], ob_recv.at[r - 1], x_line(r)).start()
    l_z_start(ly, lz, l_send, l_recv)
    for r in range(1, NX):
        drain(outb.at[0, 0], ob_recv.at[r - 1])
    remote(outb.at[c], outb.at[c], oc_send, oc_recv, core).start()
    l_x_start(lz, lx, l_send, l_recv)
    l_c_start(lx, l_send, l_recv)

    for r in range(1, NY):
        drain(mly.at[0], mlr_sem.at[r - 1])
    ml_ref[...] = mly[0] + mly[1] + mly[2] + mly[3]
    l_finish(xly, xlz, xlx, xlast_ref, xl_send, xl_recv)

    drain(outb.at[0], oc_recv)
    writes = []
    for cc in range(NC):
        for xx in range(NX):
            j = xx * NC + cc
            writes.append(pltpu.make_async_copy(
                outb.at[cc, xx], out_hbm.at[:, pl.ds(j * ds, ds)], loc_sem.at[1 + j]))
    for write in writes:
        write.start()
    l_finish(ly, lz, lx, last_ref, l_send, l_recv)
    for write in writes:
        write.wait()

    for r in range(1, NX):
        drain(mb.at[0, 0], mb_send.at[r - 1])
        drain(outb.at[0, 0], ob_send.at[r - 1])
    drain(mb.at[0], mc_send)
    drain(outb.at[0], oc_send)
    for r in range(1, NY):
        drain(mly.at[0], mls_sem.at[r - 1])
    for i in range(7):
        drain(zbuf.at[0], zs_sem.at[i])
        drain(mt.at[0], ms_sem.at[i])

    @pl.loop(0, NZ)
    def _(i):
        drain(sbuf.at[0, pl.ds(0, NQ - 1)], xs_sem.at[i])
        drain(sbuf.at[0, pl.ds(0, NQ - 1)], rs_sem.at[i])
        drain(xm.at[0, :, pl.ds(0, NX * ds)], xf_send.at[i])
        drain(ys.at[0], ys_send.at[i])

    @pl.loop(1, NZ)
    def _(i):
        drain(zbuf.at[0], ps_sem.at[i])


def layer_call(tokens, meta, gate_up, down):
    tok, width = tokens.shape
    half = down.shape[0]
    ds = width // (NX * NC)
    rows = NY * SLOTS
    seqs = NZ * NY * 4
    bf, f32 = jnp.bfloat16, jnp.float32
    dma = pltpu.SemaphoreType.DMA
    vm = pltpu.VMEM
    scratch = [
        vm((NZ, tok, ds), bf),
        vm((NC, NX, 8, 128), f32),
        vm((NZ, 24, tok), f32),
        vm((NZ, NQ, tok), f32),
        vm((NZ, NQ, tok), f32),
        vm((tok, tok), bf),
        vm((NZ, NQ, SLOTS, ds), bf),
        vm((NZ, rows, width), bf),
        vm((3, width, 2 * half // 3), bf),
        vm((NX * NC, half, ds), bf),
        vm((2 * rows, half), bf),
        vm((NZ, NX, rows, ds), bf),
        vm((NZ, NX, rows, ds), bf),
        vm((NZ, NX, rows, ds), bf),
        vm((NZ, NX, rows, ds), bf),
        vm((NZ, NQ, SLOTS, ds), bf),
        vm((NZ, tok, ds), f32),
        vm((7, tok, ds), bf),
        vm((NZ, tok, ds), bf),
        vm((NC, NX, tok, ds), bf),
        vm((NY, NY * 4, ds), bf),
        vm((NZ, NY * 4, ds), bf),
        vm((NC, NX, seqs, ds), bf),
        vm((NY, NY * 4, ds), bf),
        vm((NZ, NY * 4, ds), bf),
        vm((NC, NX, seqs, ds), bf),
        vm((NY, 24, seqs), f32),
        dma((16,)), dma((NZ,)), dma((3,)), dma((3,)), dma, dma,
        dma((7,)), dma((NZ,)), dma((7,)), dma((NZ,)),
        dma((NZ,)), dma((NZ,)), dma((NZ,)), dma((NZ,)), dma((NZ,)), dma((NZ,)),
        dma((NZ,)), dma((NZ,)), dma((NZ,)), dma((NZ,)), dma((NZ,)),
        dma((3,)), dma((3,)), dma, dma,
        dma((14,)), dma((14,)), dma((14,)), dma((14,)), dma((3,)), dma((3,)),
    ]
    anyspec = pl.BlockSpec(memory_space=pl.ANY)
    vspec = pl.BlockSpec(memory_space=pltpu.VMEM)
    return pl.pallas_call(
        layer_kernel,
        out_shape=(
            jax.ShapeDtypeStruct((tok, width), bf),
            jax.ShapeDtypeStruct((NC, NX, seqs, ds), bf),
            jax.ShapeDtypeStruct((NC, NX, seqs, ds), bf),
            jax.ShapeDtypeStruct((24, seqs), f32),
        ),
        in_specs=[anyspec, vspec, anyspec, anyspec],
        out_specs=(anyspec, vspec, vspec, vspec),
        scratch_shapes=scratch,
        compiler_params=pltpu.CompilerParams(
            collective_id=0, has_side_effects=True, vmem_limit_bytes=60 * 1024 * 1024),
        name="layer",
    )(tokens, meta, gate_up, down)


def unslice(sliced):
    cores, xs, seqs, ds = sliced.shape
    return sliced.transpose(2, 1, 0, 3).reshape(seqs, cores * xs * ds)


def body(tokens, expert_ids, gates, positives, gate_up, down):
    dp = lax.axis_index("dp")
    ex = lax.axis_index("expert")
    weight_in, weight_out = gate_up[0], down[0]
    half = weight_out.shape[0]
    meta = jnp.concatenate([
        expert_ids.astype(jnp.float32).reshape(2, 128),
        gates.reshape(2, 128),
        jnp.repeat(positives.astype(jnp.float32), tokens.shape[0] // positives.shape[0]).reshape(2, 128),
        jnp.zeros((2, 128), jnp.float32),
    ], axis=0)
    layer_out, last, xlast, ml = layer_call(tokens, meta, weight_in, weight_out)
    last = unslice(last)
    xlast = unslice(xlast)
    seqs = last.shape[0]
    values = last.astype(jnp.float32)
    norms = jnp.sqrt(jnp.sum(values * values, axis=1) + epsilon)
    unit = values / norms[:, None]
    dots = lax.dot_general(last, last, (((1,), (1,)), ((), ())), preferred_element_type=jnp.float32)
    scores = dots / (norms[:, None] * norms[None, :]) / logit_divisor
    index = jnp.arange(seqs, dtype=jnp.int32)
    exps = jnp.where(index[:, None] != index[None, :], jnp.exp(scores), 0.0)
    prob = exps / jnp.sum(exps, axis=1, keepdims=True)
    target = (index[None, :] == ml[16].astype(jnp.int32)[:, None]).astype(jnp.float32)
    coef = grad_scale * (prob - target)
    slope = jnp.dot(
        coef + coef.T, unit, precision=lax.Precision.HIGHEST, preferred_element_type=jnp.float32
    ) / logit_divisor
    proj = jnp.sum(unit * slope, axis=1, keepdims=True)
    grad_last = (slope - unit * proj) / norms[:, None]
    expert = (dp * NX + ex // NC).astype(jnp.float32)
    weight = jnp.sum(jnp.where(ml[:8] == expert, ml[8:16], 0.0), axis=0)
    route_grad = (weight[:, None] * grad_last).astype(jnp.bfloat16)
    projected = jnp.dot(xlast, weight_in, preferred_element_type=jnp.float32)
    gate_part, up_part = projected[:, :half], projected[:, half:]
    sig = jax.nn.sigmoid(gate_part)
    activated = gate_part * sig
    hidden = (activated * up_part).astype(jnp.bfloat16)
    grad_hidden = lax.dot_general(
        route_grad, weight_out, (((1,), (1,)), ((), ())), preferred_element_type=jnp.float32)
    contract = functools.partial(
        lax.dot_general, dimension_numbers=(((0,), (0,)), ((), ())),
        preferred_element_type=jnp.float32)
    grad_down = contract(hidden, route_grad).astype(jnp.bfloat16)
    slope_gate = sig * (1.0 + gate_part * (1.0 - sig))
    grad_projected = jnp.concatenate(
        [grad_hidden * up_part * slope_gate, grad_hidden * activated], axis=1
    ).astype(jnp.bfloat16)
    grad_gate_up = contract(xlast, grad_projected).astype(jnp.bfloat16)
    return layer_out, grad_gate_up[None], grad_down[None]


def solution(mesh):
    return jax.shard_map(
        body,
        mesh=mesh,
        in_specs=(
            P("dp", None),
            P("dp", "expert"),
            P("dp", "expert"),
            P("dp"),
            P(("dp", "expert"), None, None),
            P(("dp", "expert"), None, None),
        ),
        out_specs=(P("dp", None), P(("dp", "expert"), None, None), P(("dp", "expert"), None, None)),
        check_vma=False,
    )
```

time: 857 us -> 121 us (0.14)
  blocking collectives: 453 us -> 0 us
  waiting for transfers between devices: 262 us -> 0 us
  Pallas kernels: 0 us -> 99.3 us
  local copies, waits for them, and re-layouts: 72.3 us -> 5.34 us
  matrix products: 26.5 us -> 9.47 us
  between operations: 15.4 us -> 0.79 us
    all_to_all x5 -> x0, blocking collectives: 414 us -> none  [the longest x2 200 us: dispatch(): lax.all_to_all(doubled, 'dp', split_axis=0, concat_axis=0, tiled=True)]
    unnamed x3 -> x0, waiting for transfers between devices: 152 us -> none
    pallas_call x0 -> x1, Pallas kernels: none -> 99.3 us  [layer_call(): pl.pallas_call(layer_kernel, out_shape=(jax.ShapeDtypeStruct((tok, width)...]
    psum x1 -> x0, waiting for transfers between devices: 61.3 us -> none  [body(): lax.psum(contrib.astype(jnp.bfloat16), 'expert').astype(jnp.float32)]
    all_to_all x1 -> x0, waiting for transfers between devices: 48.6 us -> none  [body(): lax.all_to_all(lax.all_to_all(half_out.reshape(dp_count, expert_count, la...]
    all_gather x1 -> x0, blocking collectives: 39.1 us -> none  [body(): gathered = lax.all_gather(last_rows, 'dp', axis=0, tiled=True)]
    reshape x5 -> x0, local copies, waits for them, and re-layouts: 28 us -> none  [the longest x1 7.21 us: body(): half_out.reshape(dp_count, expert_count, lane_rows, model_width)]
    dot_general x8 -> x6, matrix products: 26.5 us -> 9.47 us  [the longest x1 2.63 us: body(): grad_gate_up = contract(xlast, grad_projected).astype(jnp.bfloat16)]
  transfers between devices with their start and end apart: 3 -> 0, of which waited for: 3 -> 0; matrix products, arithmetic and copies ran while one was open for 0% -> 0% of each run, Pallas kernels for 0% -> 0%
where the time goes in v1:
time: 121 us
  Pallas kernels  99.3 us (82%)
  matrix products  9.47 us (8%)
  other arithmetic  5.9 us (5%)
  local copies, waits for them, and re-layouts  5.34 us (4%)
    pallas_call x1, Pallas kernels, layer_call(): pl.pallas_call(layer_kernel, out_shape=(jax.ShapeDtypeStruct((tok, width)...  99.3 us
    dot_general x1, matrix products, body(): grad_gate_up = contract(xlast, grad_projected).astype(jnp.bfloat16)  2.63 us

profile of v1, /device:TPU:1, one launch (start us, length us, event | category | flops | bytes accessed | tf_op | source)
XLA Modules:
  0.0 120.8 jit_solution(17722975064307940925)
XLA Ops:
  0.6 0.7 convert_element_type.48
  1.3 0.1 broadcast_in_dim.35
  1.4 0.1 pad.5.clone
  1.5 0.1 broadcast_in_dim.36
  1.5 0.1 broadcast_in_dim.37
  1.6 0.7 convert_element_type.47
  2.3 1.3 %maximum_maximum_fusion.meta_ref = f32[8,128]{1,0:T(8,128)} fusion(f32[2,128]{1,0:T(2,128)S(1)} %broadcast_in_dim.37, f32[2,128]{1,0:T(2,128)} %bitcast.48, f32[2,128]{1,0:T(2,128)S(1)} %bitcast.47, f32[8]{0:T(128)S(1)} %pad.5.clone), kind=kLoop, calls=%fused_computation.47 | loop fusion | flops 3072 | bytes 7200 | tf_op jit(solution)/shard_map/concatenate | solution.py:457
  3.6 0.0 copy-start
  3.6 99.3 %layer.1 = (bf16[256,2048]{1,0:T(8,128)(2,1)}, bf16[2,4,128,256]{3,2,1,0:T(8,128)(2,1)}, bf16[2,4,128,256]{3,2,1,0:T(8,128)(2,1)}, f32[24,128]{1,0:T(8,128)}) custom-call(bf16[256,2048]{1,0:T(8,128)(2,1)} %tok_hbm.1, f32[8,128]{1,0:T(8,128)} %maximum_maximum_fusion.meta_ref, bf16[2048,768]{1,0:T(8,128)(2,1)} %bitcast.40, bf16[384,2048]{1,0:T(8,128)(2,1)} %bitcast.44), custom_call_target="tpu_custom_call" | custom-call | tf_op jit(solution)/shard_map/layer/pallas_call | solution.py:430
  102.9 0.7 select_reduce_fusion
  103.6 2.0 %copy.12 = bf16[128,4,2,256]{0,3,2,1:T(8,128)(2,1)} copy(bf16[128,4,2,256]{3,0,1,2:T(8,128)(2,1)} %bitcast.45) | data formatting | bytes 1048576 | tf_op jit(solution)/shard_map/transpose | solution.py:449
  105.7 0.7 convert_bitcast_fusion
  106.4 1.2 %multiply_reduce_fusion.1 = f32[128]{0:T(128)S(1)} fusion(bf16[2,4,128,256]{3,2,1,0:T(8,128)(2,1)} %get-tuple-element.10), kind=kLoop, calls=%fused_computation.7 | loop fusion | flops 786304 | bytes 524800 | tf_op jit(solution)/shard_map/reduce_sum | solution.py:468
  107.6 1.5 %fusion.2 = f32[128,128,1,1]{0,1,3,2:T(8,128)S(1)} fusion(bf16[2,4,128,256]{3,2,1,0:T(8,128)(2,1)} %get-tuple-element.10), kind=kOutput, calls=%fused_computation.8 | convolution fusion | flops 67108864 | bytes 589824 | tf_op jit(solution)/shard_map/dot_general | solution.py:470
  109.1 0.0 copy-start.7
  109.1 0.1 copy.15
  109.2 0.5 copy-done.7
  109.7 0.0 copy-start.5
  109.7 0.6 copy-done.5
  110.4 0.0 copy-start.2
  110.4 0.2 fusion.42
  110.6 0.0 copy-done
  110.6 1.7 %fusion.35 = f32[128,768]{1,0:T(8,128)S(1)} fusion(bf16[128,2048]{0,1:T(8,128)(2,1)} %bitcast.41, bf16[1,2048,768]{2,1,0:T(8,128)(2,1)S(1)} %copy-done), kind=kOutput, calls=%fused_computation.56 | convolution fusion | flops 402653184 | bytes 4063232 | tf_op jit(solution)/shard_map/dot_general | solution.py:485
  112.2 0.0 copy-done.2
  112.3 0.0 copy-start.6
  112.3 0.0 copy-start.8
  112.3 0.1 bitcast_convert_fusion
  112.4 0.3 copy.16
  112.7 0.3 copy.17
  113.0 0.0 copy-done.6
  113.1 0.0 copy-done.8
  113.1 0.0 copy-start.3
  113.1 1.3 %multiply_reduce_fusion = (f32[128]{0:T(128)S(1)}, f32[128,2048]{1,0:T(8,128)S(1)}) fusion(f32[128,2048]{1,0:T(8,128)S(1)} %copy.17, f32[128]{0:T(128)S(1)} %add_sqrt_fusion, f32[128,128,1,1]{0,1,3,2:T(8,128)S(1)} %copy-done.8, s32[128]{0:T(128)S(1)} %convert_bitcast_fusion, f32[128]{0:T(128)S(1)} %fusion.42, f32[128,128]{1,0:T(8,128)S(1)} %copy-done.6), kind=kOutput, calls=%fused_computation.6 | convolution fusion | flops 404275072 | bytes 2230272 | tf_op jit(solution)/shard_map/dot_general | solution.py:477
  114.4 0.3 multiply_convert_fusion
  114.8 0.0 copy-done.3
  114.8 0.0 copy-start.1
  114.8 0.6 multiply_convert_fusion.3
  115.4 0.0 copy-start.4
  115.4 1.8 %fusion.1 = bf16[1,384,2048]{2,1,0:T(8,128)(2,1)} fusion(bf16[128,2048]{1,0:T(8,128)(2,1)S(1)} %multiply_convert_fusion, f32[128,768]{1,0:T(8,128)S(1)} %fusion.35), kind=kOutput, calls=%fused_computation.3 | convolution fusion | flops 202407936 | bytes 2490368 | tf_op jit(solution)/shard_map/dot_general | solution.py:495
  117.2 0.0 copy-done.1
  117.2 2.6 %fusion = bf16[1,2048,768]{2,1,0:T(8,128)(2,1)} fusion(bf16[128,2048]{0,1:T(8,128)(2,1)S(1)} %bitcast.42, bf16[128,384]{1,0:T(8,128)(2,1)S(1)} %get-tuple-element.12, bf16[128,384]{1,0:T(8,128)(2,1)S(1)} %get-tuple-element.11), kind=kOutput, calls=%fused_computation.1 | convolution fusion | flops 404619264 | bytes 3866624 | tf_op jit(solution)/shard_map/dot_general | solution.py:500
  119.8 0.0 copy-done.4
  119.8 1.0 copy.22
  (2 shorter events, 0.0 us)
Async XLA Ops:
  3.6 106.9 %copy-start = (bf16[1,2048,768]{2,1,0:T(8,128)(2,1)S(1)}, bf16[1,2048,768]{2,1,0:T(8,128)(2,1)}, u32[]{:S(2)}) copy-start(bf16[1,2048,768]{2,1,0:T(8,128)(2,1)} %param.10) | copy-start | bytes 9437188
  109.1 0.6 copy-start.7
  109.7 0.6 copy-start.5
  110.4 1.9 %copy-start.2 = (bf16[2,4,128,256]{3,2,1,0:T(8,128)(2,1)S(1)}, bf16[2,4,128,256]{3,2,1,0:T(8,128)(2,1)}, u32[]{:S(2)}) copy-start(bf16[2,4,128,256]{3,2,1,0:T(8,128)(2,1)} %get-tuple-element.10) | copy-start | bytes 1572868
  112.3 0.8 copy-start.6
  112.3 0.9 copy-start.8
  113.1 1.7 %copy-start.3 = (bf16[1,384,2048]{2,1,0:T(8,128)(2,1)S(1)}, bf16[1,384,2048]{2,1,0:T(8,128)(2,1)}, u32[]{:S(2)}) copy-start(bf16[1,384,2048]{2,1,0:T(8,128)(2,1)} %param.11) | copy-start | bytes 4718596
  114.8 2.4 %copy-start.1 = (bf16[128,4,2,256]{0,3,2,1:T(8,128)(2,1)S(1)}, bf16[128,4,2,256]{0,3,2,1:T(8,128)(2,1)}, u32[]{:S(2)}) copy-start(bf16[128,4,2,256]{0,3,2,1:T(8,128)(2,1)} %copy.12) | copy-start | bytes 1572868
  115.4 4.4 %copy-start.4 = (bf16[256,2048]{1,0:T(8,128)(2,1)S(1)}, bf16[256,2048]{1,0:T(8,128)(2,1)}, u32[]{:S(2)}) copy-start(bf16[256,2048]{1,0:T(8,128)(2,1)} %get-tuple-element.18) | copy-start | bytes 3145732

commit v2 on v1

v2 whole, which is shorter than its diff:
```python
import functools

import jax
import jax.numpy as jnp
from jax import lax
from jax.experimental import pallas as pl
from jax.experimental.pallas import tpu as pltpu
from jax.sharding import PartitionSpec as P

logit_divisor = 0.05
grad_scale = 256.0
epsilon = 1e-06

MESH = pl.DeviceIdType.MESH
NZ, NY, NX, NC = 8, 4, 4, 2
NQ = NY * NX
SLOTS = 32


def layer_kernel(
    tok_hbm, ids_ref, gates_ref, pos_ref, gu_hbm, dn_hbm,
    out_hbm, xlast_hbm, hid_hbm, rg_hbm, gp_hbm,
    zbuf, tokc, mb, mo, mt, rk, gw, tri, sbuf, xm, gu, dn, hid, ys, yo, yr, rs, rbuf, prec, psend, pacc, outb,
    xly, mly, xlz, mlz, plast, kls, klo, klr, kz, kzr, ky, kx, lastz, xlast_ref, hid_ref, rg_ref, gp_ref,
    loc_sem, own_sem, mb_send, mb_recv, zs_sem, zr_sem, ms_sem, mr_sem,
    xs_sem, xr_sem, xf_send, xf_recv, ys_send, ys_recv, rs_sem, rr_sem, rown_sem, ps_sem, pr_sem,
    ob_send, ob_recv, oc_send, oc_recv,
    xly_send, xly_recv, mly_send, mly_recv, xlz_send, xlz_recv, mlz_send, mlz_recv,
    xlc_send, xlc_recv, klc_send, klc_recv, kz_send, kz_recv, ky_send, ky_recv, kx_send, kx_recv,
    lz_send, lz_recv, lc_send, lc_recv, out_sem,
):
    dp = lax.axis_index("dp")
    ex = lax.axis_index("expert")
    z, y, x, c = dp // NY, dp % NY, ex // NC, ex % NC
    q_me = y * NX + x
    tok, ds = zbuf.shape[1], zbuf.shape[2]
    rows = NY * SLOTS
    hw = NX * ds
    seqs = plast.shape[0]
    per = seqs // (NZ * NY)
    length = tok // per
    core = (dp, x * NC + (1 - c))
    f32, bf = jnp.float32, jnp.bfloat16

    def at(zz, yy, xx):
        return (zz * NY + yy, xx * NC + c)

    def z_line(r):
        return at((z + r) % NZ, y, x)

    def y_line(r):
        return at(z, (y + r) % NY, x)

    def x_line(r):
        return at(z, y, (x + r) % NX)

    def group(r):
        return (dp, (ex + r) % (NX * NC))

    def plane(r):
        q = (q_me + r) % NQ
        return q, at(z, q // NX, q % NX)

    def plane_of(i):
        return (z + ((i + 1) // 2) * (2 * (i % 2) - 1) + NZ) % NZ

    def remote(src, dst, send, recv, device):
        return pltpu.make_async_remote_copy(
            src_ref=src, dst_ref=dst, send_sem=send, recv_sem=recv,
            device_id=device, device_id_type=MESH,
        )

    def drain(ref, sem):
        pltpu.make_async_copy(ref, ref, sem).wait()

    def signal(device):
        pl.semaphore_signal(barrier, inc=1, device_id=device, device_id_type=MESH)

    half = hid.shape[1]
    nch = gu.shape[0]
    ch = half // nch
    col_me = pl.multiple_of(ex * ds, ds)
    tok_load = pltpu.make_async_copy(tok_hbm.at[:, pl.ds(col_me, ds)], zbuf.at[0], loc_sem.at[0])
    tok_load.start()
    tok_loads = [
        pltpu.make_async_copy(
            tok_hbm.at[:, pl.ds(pl.multiple_of((xx * NC + c) * ds, ds), ds)], tokc.at[xx],
            loc_sem.at[1 + xx])
        for xx in range(NX)
    ]
    for load in tok_loads:
        load.start()
    loads = []
    for n in range(nch):
        for part in range(2):
            loads.append(pltpu.make_async_copy(
                gu_hbm.at[:, pl.ds(part * half + n * ch, ch)],
                gu.at[n, :, pl.ds(part * ch, ch)], loc_sem.at[5 + 2 * n + part]))
    for j in range(NX * NC):
        loads.append(pltpu.make_async_copy(
            dn_hbm.at[:, pl.ds(j * ds, ds)], dn.at[j], loc_sem.at[5 + 2 * nch + j]))

    for load in loads:
        load.start()

    barrier = pltpu.get_barrier_semaphore()

    @pl.loop(1, NZ)
    def _(r):
        signal(z_line(r))

    @pl.loop(1, NQ)
    def _(r):
        signal(plane(r)[1])

    signal(core)
    for r in range(1, NX):
        signal((dp, (x + r) % NX * NC + (1 - c)))

    lane = lax.broadcasted_iota(jnp.int32, (1, 128), 1)
    mb[c, x, 0:2, :] = ids_ref[...].astype(f32)
    mb[c, x, 2:4, :] = gates_ref[...]
    mb[c, x, 4:5, :] = jnp.where(lane < length, pos_ref[0], pos_ref[1]).astype(f32)
    mb[c, x, 5:6, :] = jnp.where(lane < length, pos_ref[2], pos_ref[3]).astype(f32)
    mb[c, x, 6:8, :] = jnp.zeros((2, 128), f32)
    ti = lax.broadcasted_iota(jnp.int32, (tok, tok), 0)
    tj = lax.broadcasted_iota(jnp.int32, (tok, tok), 1)
    tri[...] = jnp.where(ti < tj, 1.0, 0.0).astype(bf)

    lrow = lax.broadcasted_iota(jnp.int32, (NY * per, tok), 0)
    ltok = lax.broadcasted_iota(jnp.int32, (NY * per, tok), 1)
    last_sel = jnp.where(
        (ltok % length == length - 1) & (lrow == y * per + ltok // length), 1.0, 0.0)
    for load in tok_loads:
        load.wait()
    for xx in range(NX):
        xly[y, :, xx * ds:(xx + 1) * ds] = jnp.dot(
            last_sel.astype(bf), tokc[xx], preferred_element_type=f32).astype(bf)
    mly[y] = jnp.zeros((NY * per, 128), f32)
    tok_load.wait()
    pl.semaphore_wait(barrier, NZ + NQ - 1 + NX - 1)

    for r in range(1, NX * NC):
        remote(mb.at[c, x], mb.at[c, x], mb_send.at[r - 1], mb_recv.at[r - 1], group(r)).start()

    up, down = z_line(1), z_line(NZ - 1)

    def ring_own(view, down_view, up_view, send, recv):
        remote(view, down_view, send.at[6], recv.at[1], down).start()
        remote(view, up_view, send.at[0], recv.at[2], up).start()

    def ring_on(i, view, next_view, send, recv):
        device = at((z + 1 - 2 * (i % 2) + NZ) % NZ, y, x)
        remote(view, next_view, send.at[i], recv.at[i + 2], device).start()

    ring_own(zbuf.at[0], zbuf.at[1], zbuf.at[2], zs_sem, zr_sem)
    for r in range(1, NY):
        remote(xly.at[y], xly.at[y], xly_send.at[r - 1], xly_recv.at[r - 1], y_line(r)).start()

    for r in range(1, NX * NC):
        drain(mb.at[0, 0], mb_recv.at[r - 1])
    for side in range(2):
        cols = slice(side * 128, (side + 1) * 128)
        for part in range(2):
            for cc in range(NC):
                mo[part * 8 + cc * NX:part * 8 + (cc + 1) * NX, cols] = mb[cc, :, 2 * part + side, :]
        mo[16:24, cols] = jnp.broadcast_to(mb[0, 0, 4 + side:5 + side, :], (8, 128))
    mt[0] = mo[0:16, :].astype(bf)
    ring_own(mt.at[0], mt.at[1], mt.at[2], ms_sem, mr_sem)

    slot_iota = lax.broadcasted_iota(jnp.int32, (SLOTS, tok), 0).astype(f32)

    def gather_block(i):
        table = mt[i].astype(f32)
        ids, gate = table[0:8], table[8:16]
        hits, weights = [], []
        for q in range(NQ):
            hit = ids == (z * NQ + q).astype(f32)
            hits.append(jnp.sum(jnp.where(hit, 1.0, 0.0), axis=0, keepdims=True))
            weights.append(jnp.sum(jnp.where(hit, gate, 0.0), axis=0, keepdims=True))
        hit = jnp.concatenate(hits, axis=0)
        rank = jnp.dot(hit.astype(bf), tri[...], preferred_element_type=f32)
        ranked = jnp.where(hit > 0.0, rank, -1.0)
        rk[i] = ranked
        gw[i] = jnp.concatenate(weights, axis=0)
        picks = jnp.concatenate(
            [jnp.where(slot_iota == ranked[q:q + 1, :], 1.0, 0.0) for q in range(NQ)], axis=0
        ).astype(bf)
        got = jnp.dot(picks, zbuf[i], preferred_element_type=f32)
        sbuf[i] = got.astype(bf).reshape(NQ, SLOTS, ds)

        def place():
            return xm.at[i, pl.ds(pl.multiple_of(y * SLOTS, SLOTS), SLOTS), pl.ds(col_me, ds)]

        @pl.loop(1, NQ)
        def _(r):
            q, device = plane(r)
            remote(sbuf.at[i, q], place(), xs_sem.at[i], xr_sem.at[i], device).start()

        pltpu.make_async_copy(sbuf.at[i, q_me], place(), own_sem.at[i]).start()

    gather_block(0)

    mly[y, :, 0:24] = lax.dot_general(
        last_sel, mo[...], (((1,), (1,)), ((), ())), precision=lax.Precision.HIGHEST,
        preferred_element_type=f32)
    for r in range(1, NY):
        remote(mly.at[y], mly.at[y], mly_send.at[r - 1], mly_recv.at[r - 1], y_line(r)).start()
    def last_rows_own():
        for r in range(1, NY):
            drain(xly.at[0], xly_recv.at[r - 1])
        total = xly[0].astype(f32)
        for r in range(1, NY):
            total += xly[r].astype(f32)
        xlz[c, z] = total.astype(bf)
        for r in range(1, NY):
            drain(mly.at[0], mly_recv.at[r - 1])
        mlz[z] = mly[0] + mly[1] + mly[2] + mly[3]
        for r in range(1, NZ):
            remote(xlz.at[c, z], xlz.at[c, z], xlz_send.at[r - 1], xlz_recv.at[r - 1],
                   z_line(r)).start()
            remote(mlz.at[z], mlz.at[z], mlz_send.at[r - 1], mlz_recv.at[r - 1], z_line(r)).start()

    def forward(i):
        drain(sbuf.at[0, pl.ds(0, NQ - 1)], xr_sem.at[i])
        drain(sbuf.at[0, 0], own_sem.at[i])
        for xx in range(NX):
            cols = pl.ds(pl.multiple_of((xx * NC + c) * ds, ds), ds)
            remote(xm.at[i, :, cols], xm.at[i, :, cols], xf_send.at[i], xf_recv.at[i], core).start()

    def silu_mul(pr):
        g, u = pr[:, :ch], pr[:, ch:]
        return (g * jax.nn.sigmoid(g) * u).astype(bf)

    def experts(p):
        for b in range(2):
            drain(xm.at[0, :, pl.ds(0, hw)], xf_recv.at[2 * p + b])
        xrows = xm[pl.ds(2 * p, 2)].reshape(2 * rows, NC * hw)
        for n in range(nch):
            hid[:, n * ch:(n + 1) * ch] = silu_mul(
                jnp.dot(xrows, gu[n], preferred_element_type=f32))
        hv = hid[...]
        for xx in range(NX):
            o = jnp.dot(hv, dn[xx * NC + 1 - c], preferred_element_type=f32).astype(bf)
            ys[2 * p, xx] = o[:rows]
            ys[2 * p + 1, xx] = o[rows:]
        for b in range(2):
            remote(ys.at[2 * p + b], yr.at[2 * p + b], ys_send.at[2 * p + b],
                   ys_recv.at[2 * p + b], core).start()
        for xx in range(NX):
            o = jnp.dot(hv, dn[xx * NC + c], preferred_element_type=f32).astype(bf)
            yo[2 * p, xx] = o[:rows]
            yo[2 * p + 1, xx] = o[rows:]

    def all_columns(buf, j):
        part = buf[j % NC, :, :, (j // NC) * ds:(j // NC + 1) * ds]
        return part.reshape(seqs, ds)

    def experts_last():
        drain(xlz.at[0], xlc_recv)
        xrows = jnp.concatenate([all_columns(xlz, j) for j in range(NX * NC)], axis=1)
        for n in range(nch):
            pr = jnp.dot(xrows, gu[n], preferred_element_type=f32)
            plast[:, 2 * n * ch:2 * (n + 1) * ch] = pr
            hid[:seqs, n * ch:(n + 1) * ch] = silu_mul(pr)
        hv = hid[:seqs]
        hid_ref[...] = hv.astype(f32).T.astype(bf)
        for xx in range(NX):
            o = jnp.dot(hv, dn[xx * NC + 1 - c], preferred_element_type=f32).astype(bf)
            kls[:, :, xx * ds:(xx + 1) * ds] = o.reshape(NZ, NY * per, ds)
        remote(kls, klr, klc_send, klc_recv, core).start()
        for xx in range(NX):
            o = jnp.dot(hv, dn[xx * NC + c], preferred_element_type=f32).astype(bf)
            klo[:, :, xx * ds:(xx + 1) * ds] = o.reshape(NZ, NY * per, ds)

    lanes = lax.broadcasted_iota(jnp.int32, (seqs, 128), 1)

    def last_weight():
        m = mlz[...].reshape(seqs, 128)
        mine = (m == (dp * NX + x).astype(f32)) & (lanes < 8)
        return jnp.sum(jnp.where(mine, pltpu.roll(m, 120, 1), 0.0), axis=1, keepdims=True)

    def last_to_planes():
        drain(klr, klc_recv)
        both = klo[...].astype(f32) + klr[...].astype(f32)
        kz[...] = (both.reshape(seqs, hw) * last_weight()).astype(bf).reshape(NZ, NY * per, hw)
        for r in range(1, NZ):
            remote(kz.at[(z + r) % NZ], kzr.at[z], kz_send.at[r - 1], kz_recv.at[r - 1],
                   z_line(r)).start()

    def last_to_y():
        for r in range(1, NZ):
            drain(kz.at[0], kz_recv.at[r - 1])
        total = kz[z].astype(f32)
        for r in range(1, NZ):
            total += kzr[(z + r) % NZ].astype(f32)
        ky[y] = total.astype(bf)
        for r in range(1, NY):
            remote(ky.at[y], ky.at[y], ky_send.at[r - 1], ky_recv.at[r - 1], y_line(r)).start()

    def last_to_x():
        for r in range(1, NY):
            drain(ky.at[0], ky_recv.at[r - 1])
        total = ky[0].astype(f32)
        for r in range(1, NY):
            total += ky[r].astype(f32)
        kx[x] = total.astype(bf)
        for r in range(1, NX):
            remote(kx.at[x], kx.at[x], kx_send.at[r - 1], kx_recv.at[r - 1], x_line(r)).start()

    def last_to_all():
        for r in range(1, NX):
            drain(kx.at[0], kx_recv.at[r - 1])
        total = kx[0].astype(f32)
        for r in range(1, NX):
            total += kx[r].astype(f32)
        lastz[c, z] = (xlz[c, z].astype(f32) + total).astype(bf)
        for r in range(1, NZ):
            remote(lastz.at[c, z], lastz.at[c, z], lz_send.at[r - 1], lz_recv.at[r - 1],
                   z_line(r)).start()

    def last_to_core():
        for r in range(1, NZ):
            drain(kz.at[0], lz_recv.at[r - 1])
        remote(lastz.at[c], lastz.at[c], lc_send, lc_recv, core).start()

    def loss_and_rows():
        drain(lastz.at[0], lc_recv)
        dots = jnp.zeros((seqs, seqs), f32)
        for cc in range(NC):
            part = lastz[cc].reshape(seqs, hw)
            dots += lax.dot_general(
                part, part, (((1,), (1,)), ((), ())), preferred_element_type=f32)
        ri = lax.broadcasted_iota(jnp.int32, (seqs, seqs), 0)
        cj = lax.broadcasted_iota(jnp.int32, (seqs, seqs), 1)
        eye = ri == cj
        squares = jnp.where(eye, dots, 0.0)
        n_col = jnp.sqrt(jnp.sum(squares, axis=1, keepdims=True) + epsilon)
        n_row = jnp.sqrt(jnp.sum(squares, axis=0, keepdims=True) + epsilon)
        scores = dots / (n_col * n_row) / logit_divisor
        exps = jnp.where(eye, 0.0, jnp.exp(scores))
        prob = exps / jnp.sum(exps, axis=1, keepdims=True)
        m = mlz[...].reshape(seqs, 128)
        positive = jnp.sum(jnp.where(lanes == 16, m, 0.0), axis=1, keepdims=True)
        coef = grad_scale * (prob - jnp.where(cj.astype(f32) == positive, 1.0, 0.0))
        both = coef + coef.T
        proj = jnp.sum(both * scores, axis=1, keepdims=True)
        mat = (both / (n_row * logit_divisor) - jnp.where(eye, proj / n_col, 0.0)) / n_col
        mat = mat * last_weight()
        first = mat.astype(bf)
        rest = mat - first.astype(f32)
        second = rest.astype(bf)
        third = (rest - second.astype(f32)).astype(bf)
        grad_hidden = jnp.zeros((seqs, half), f32)
        for j in range(NX * NC):
            lj = all_columns(lastz, j)
            g = jnp.dot(first, lj, preferred_element_type=f32)
            g += jnp.dot(second, lj, preferred_element_type=f32)
            g += jnp.dot(third, lj, preferred_element_type=f32)
            g = g.astype(bf)
            rg_ref[:, j * ds:(j + 1) * ds] = g
            xlast_ref[j * ds:(j + 1) * ds, :] = all_columns(xlz, j).astype(f32).T.astype(bf)
            grad_hidden += lax.dot_general(
                g, dn[j], (((1,), (1,)), ((), ())), preferred_element_type=f32)
        for n in range(nch):
            gate_part = plast[:, 2 * n * ch:(2 * n + 1) * ch]
            up_part = plast[:, (2 * n + 1) * ch:2 * (n + 1) * ch]
            gh = grad_hidden[:, n * ch:(n + 1) * ch]
            sig = jax.nn.sigmoid(gate_part)
            gp_ref[:, n * ch:(n + 1) * ch] = (
                gh * up_part * (sig * (1.0 + gate_part * (1.0 - sig)))).astype(bf)
            gp_ref[:, half + n * ch:half + (n + 1) * ch] = (gh * (gate_part * sig)).astype(bf)

    def swap_last_rows():
        for r in range(NZ - 1):
            drain(xlz.at[0, 0], xlz_recv.at[r])
            drain(mlz.at[0], mlz_recv.at[r])
        remote(xlz.at[c], xlz.at[c], xlc_send, xlc_recv, core).start()

    def send_back(i):
        drain(ys.at[0], ys_recv.at[i])
        rs[i] = (yo[i].astype(f32) + yr[i].astype(f32)).astype(bf)

        def piece(q):
            return rs.at[i, q % NX, pl.ds(pl.multiple_of((q // NX) * SLOTS, SLOTS), SLOTS)]

        @pl.loop(1, NQ)
        def _(r):
            q, device = plane(r)
            remote(piece(q), rbuf.at[i, q_me], rs_sem.at[i], rr_sem.at[i], device).start()

        pltpu.make_async_copy(piece(q_me), rbuf.at[i, q_me], rown_sem.at[i]).start()

    @pl.loop(1, 11)
    def _(i):
        @pl.when((i == 7) | (i == 9) | (i == 10))
        def _():
            experts((i - 7) // 2 + (i // 10))

        @pl.when(i < NZ)
        def _():
            drain(zbuf.at[0], zr_sem.at[i])
            drain(mt.at[0], mr_sem.at[i])

            @pl.when(i <= 5)
            def _():
                ring_on(i, zbuf.at[i], zbuf.at[i + 2], zs_sem, zr_sem)
                ring_on(i, mt.at[i], mt.at[i + 2], ms_sem, mr_sem)

            gather_block(i)

        @pl.when(i >= 5)
        def _():
            forward(i - 5 + (i + 1) // 8 + i // 10)

        @pl.when((i == 6) | (i == 9))
        def _():
            forward(2 + 4 * (i // 9))

        @pl.when(i == 5)
        def _():
            for load in loads:
                load.wait()

        @pl.when(i == 6)
        def _():
            last_rows_own()

        @pl.when(i == 9)
        def _():
            swap_last_rows()

    send_back(5)
    send_back(4)
    experts_last()
    experts(NZ // 2 - 1)
    last_to_planes()

    def arrived(i):
        drain(sbuf.at[0, pl.ds(0, NQ - 1)], rr_sem.at[i])
        drain(sbuf.at[0, 0], rown_sem.at[i])

    def combine(i):
        ranked, w = rk[i], gw[i]
        spread = jnp.concatenate(
            [jnp.where(slot_iota == ranked[q:q + 1, :], w[q:q + 1, :], 0.0) for q in range(NQ)],
            axis=0,
        ).astype(bf)
        return lax.dot_general(
            spread, rbuf[i].reshape(NQ * SLOTS, ds), (((0,), (0,)), ((), ())),
            preferred_element_type=f32)


    row_copies = [
        pltpu.make_async_copy(src, dst, out_sem.at[8 + n]) for n, (src, dst) in enumerate((
            (xlast_ref, xlast_hbm), (hid_ref, hid_hbm), (rg_ref, rg_hbm), (gp_ref, gp_hbm)))]

    def drained_early():
        for r in range(NX * NC - 1):
            drain(mb.at[0, 0], mb_send.at[r])
        for r in range(NY - 1):
            drain(xly.at[0], xly_send.at[r])
            drain(mly.at[0], mly_send.at[r])
        for r in range(NZ - 1):
            drain(zbuf.at[0], zs_sem.at[r])
            drain(mt.at[0], ms_sem.at[r])
            drain(xlz.at[0, 0], xlz_send.at[r])
            drain(mlz.at[0], mlz_send.at[r])
        drain(xlz.at[0], xlc_send)
        drain(kls, klc_send)
        for n in range(NZ):
            drain(sbuf.at[0, pl.ds(0, NQ - 1)], xs_sem.at[n])
            drain(xm.at[0, :, pl.ds(0, hw)], xf_send.at[n])

    def order(n):
        return NZ - 1 - n + (1 - n // 4) * (4 * (n // 2 % 2) - 2)

    def sum_on(i):
        slot = (i + 5) % 7
        device = at((z - 1 + 2 * (i % 2) + NZ) % NZ, y, x)
        remote(psend.at[i], prec.at[slot], ps_sem.at[i], pr_sem.at[slot], device).start()

    def add_on(i):
        drain(prec.at[0], pr_sem.at[i])
        psend[i] = (pacc[i - 4] + prec[i].astype(f32)).astype(bf)
        sum_on(i)

    @pl.loop(0, NZ - 1)
    def _(n):
        i = order(n)
        arrived(i)

        @pl.when(n <= NZ - 3)
        def _():
            send_back(order(n + 2))

        part = combine(i)

        @pl.when(n < 2)
        def _():
            pacc[1 - n] = part

        @pl.when((n >= 2) & (n < 4))
        def _():
            psend[i] = part.astype(bf)
            sum_on(i)

        @pl.when(n == 3)
        def _():
            add_on(5)

        @pl.when(n == 4)
        def _():
            add_on(4)

        @pl.when(n >= 4)
        def _():
            drain(prec.at[0], pr_sem.at[i])
            psend[i] = (part + prec[i].astype(f32)).astype(bf)
            sum_on(i)

        @pl.when(n == 0)
        def _():
            drained_early()

        @pl.when(n == 2)
        def _():
            last_to_y()

        @pl.when(n == 4)
        def _():
            last_to_x()

        @pl.when(n == 6)
        def _():
            last_to_all()

    arrived(0)
    part = combine(0)
    drain(prec.at[0], pr_sem.at[0])
    drain(prec.at[0], pr_sem.at[6])
    part += prec[0].astype(f32) + prec[6].astype(f32)
    outb[c, x] = (zbuf[0].astype(f32) + part).astype(bf)
    remote(outb.at[c, x], outb.at[c, x], oc_send.at[0], oc_recv.at[0], core).start()
    for r in range(1, NX):
        remote(outb.at[c, x], outb.at[c, x], ob_send.at[r - 1], ob_recv.at[r - 1], x_line(r)).start()
    out_copies = [pltpu.make_async_copy(outb.at[c, x], out_hbm.at[c, x], out_sem.at[0])]
    out_copies[-1].start()
    for r in range(NX - 1):
        drain(kx.at[0], kx_send.at[r])
        drain(ky.at[0], ky_send.at[r])
    for r in range(NZ - 1):
        drain(kz.at[0], kz_send.at[r])
    for i in range(NZ):
        drain(ys.at[0], ys_send.at[i])
    for i in range(1, NZ):
        drain(sbuf.at[0, pl.ds(0, NQ - 1)], rs_sem.at[i])
    def spread_out(r):
        xx = (x + NX - r) % NX
        drain(outb.at[0, 0], ob_recv.at[r - 1])
        remote(outb.at[c, xx], outb.at[c, xx], oc_send.at[r], oc_recv.at[r], core).start()
        out_copies.append(pltpu.make_async_copy(outb.at[c, xx], out_hbm.at[c, xx], out_sem.at[r]))
        out_copies[-1].start()

    def take_out(r):
        xx = (x + NX - r) % NX
        drain(outb.at[0, 0], oc_recv.at[r])
        out_copies.append(pltpu.make_async_copy(
            outb.at[1 - c, xx], out_hbm.at[1 - c, xx], out_sem.at[4 + r]))
        out_copies[-1].start()

    take_out(0)
    last_to_core()
    spread_out(1)
    spread_out(3)
    loss_and_rows()
    for copy in row_copies:
        copy.start()
    spread_out(2)
    for r in range(1, NX):
        take_out(r)

    for r in range(NX - 1):
        drain(outb.at[0, 0], ob_send.at[r])
    for r in range(NX):
        drain(outb.at[0, 0], oc_send.at[r])
    for i in range(1, NZ):
        drain(zbuf.at[0], ps_sem.at[i])
    drain(sbuf.at[0, pl.ds(0, NQ - 1)], rs_sem.at[0])
    for r in range(NZ - 1):
        drain(kz.at[0], lz_send.at[r])
    drain(lastz.at[0], lc_send)
    for copy in row_copies:
        copy.wait()
    for copy in out_copies:
        copy.wait()


def layer_call(tokens, ids, gates, positives, gate_up, down):
    tok, width = tokens.shape
    half = down.shape[0]
    ds = width // (NX * NC)
    hw = NX * ds
    rows = NY * SLOTS
    per = positives.shape[0]
    seqs = NZ * NY * per
    bf, f32 = jnp.bfloat16, jnp.float32
    dma = pltpu.SemaphoreType.DMA
    vm = pltpu.VMEM
    scratch = [
        vm((NZ, tok, ds), bf),
        vm((NX, tok, ds), bf),
        vm((NC, NX, 8, 128), f32),
        vm((24, tok), f32),
        vm((NZ, 16, tok), bf),
        vm((NZ, NQ, tok), f32),
        vm((NZ, NQ, tok), f32),
        vm((tok, tok), bf),
        vm((NZ, NQ, SLOTS, ds), bf),
        vm((NZ, rows, width), bf),
        vm((3, width, 2 * half // 3), bf),
        vm((NX * NC, half, ds), bf),
        vm((2 * rows, half), bf),
        vm((NZ, NX, rows, ds), bf),
        vm((NZ, NX, rows, ds), bf),
        vm((NZ, NX, rows, ds), bf),
        vm((NZ, NX, rows, ds), bf),
        vm((NZ, NQ, SLOTS, ds), bf),
        vm((7, tok, ds), bf),
        vm((NZ, tok, ds), bf),
        vm((2, tok, ds), f32),
        vm((NC, NX, tok, ds), bf),
        vm((NY, NY * per, hw), bf),
        vm((NY, NY * per, 128), f32),
        vm((NC, NZ, NY * per, hw), bf),
        vm((NZ, NY * per, 128), f32),
        vm((seqs, 2 * half), f32),
        vm((NZ, NY * per, hw), bf),
        vm((NZ, NY * per, hw), bf),
        vm((NZ, NY * per, hw), bf),
        vm((NZ, NY * per, hw), bf),
        vm((NZ, NY * per, hw), bf),
        vm((NY, NY * per, hw), bf),
        vm((NX, NY * per, hw), bf),
        vm((NC, NZ, NY * per, hw), bf),
        vm((width, seqs), bf),
        vm((half, seqs), bf),
        vm((seqs, width), bf),
        vm((seqs, 2 * half), bf),
        dma((20,)), dma((NZ,)), dma((7,)), dma((7,)),
        dma((7,)), dma((NZ,)), dma((7,)), dma((NZ,)),
        dma((NZ,)), dma((NZ,)), dma((NZ,)), dma((NZ,)), dma((NZ,)), dma((NZ,)),
        dma((NZ,)), dma((NZ,)), dma((NZ,)), dma((NZ,)), dma((NZ,)),
        dma((3,)), dma((3,)), dma((NX,)), dma((NX,)),
        dma((3,)), dma((3,)), dma((3,)), dma((3,)), dma((7,)), dma((NZ,)), dma((7,)), dma((NZ,)),
        dma, dma, dma, dma, dma((7,)), dma((7,)), dma((3,)), dma((3,)), dma((3,)), dma((3,)),
        dma((7,)), dma((7,)), dma, dma, dma((12,)),
    ]
    anyspec = pl.BlockSpec(memory_space=pl.ANY)
    vspec = pl.BlockSpec(memory_space=pltpu.VMEM)
    sspec = pl.BlockSpec(memory_space=pltpu.SMEM)
    return pl.pallas_call(
        layer_kernel,
        out_shape=(
            jax.ShapeDtypeStruct((NC, NX, tok, ds), bf),
            jax.ShapeDtypeStruct((width, seqs), bf),
            jax.ShapeDtypeStruct((half, seqs), bf),
            jax.ShapeDtypeStruct((seqs, width), bf),
            jax.ShapeDtypeStruct((seqs, 2 * half), bf),
        ),
        in_specs=[anyspec, vspec, vspec, sspec, anyspec, anyspec],
        out_specs=(anyspec,) * 5,
        scratch_shapes=scratch,
        compiler_params=pltpu.CompilerParams(
            collective_id=0, has_side_effects=True, vmem_limit_bytes=60 * 1024 * 1024),
        name="layer",
    )(tokens, ids, gates, positives, gate_up, down)


def finish_kernel(
    out_hbm, xlast_hbm, hid_hbm, rg_hbm, gp_hbm, layer_hbm, ggu_hbm, gd_hbm,
    out_v, xlast_v, hid_v, rg_v, gp_v, ggu_v, gd_v, in_sem, out_sem,
):
    tok, ds = out_v.shape[2], out_v.shape[3]
    reads = [
        pltpu.make_async_copy(src, dst, in_sem.at[n])
        for n, (src, dst) in enumerate((
            (gp_hbm, gp_v), (xlast_hbm, xlast_v), (rg_hbm, rg_v), (hid_hbm, hid_v),
            (out_hbm, out_v)))
    ]
    for read in reads:
        read.start()
    steps = NX * NC
    rows = xlast_v.shape[0] // steps
    hrows = hid_v.shape[0] // 3
    reads[0].wait()
    reads[1].wait()

    def ggu_out(n):
        part = pl.ds(pl.multiple_of(n * rows, rows), rows)
        return pltpu.make_async_copy(ggu_v.at[part], ggu_hbm.at[0, part], out_sem.at[n])

    @pl.loop(0, steps)
    def _(n):
        part = pl.ds(pl.multiple_of(n * rows, rows), rows)
        ggu_v[part] = jnp.dot(
            xlast_v[part], gp_v[...], preferred_element_type=jnp.float32).astype(jnp.bfloat16)
        ggu_out(n).start()

    for read in reads[2:]:
        read.wait()
    layer_out = [
        pltpu.make_async_copy(
            out_v.at[j % NC, j // NC], layer_hbm.at[:, pl.ds(j * ds, ds)], out_sem.at[steps + j])
        for j in range(steps)
    ]
    for copy in layer_out:
        copy.start()
    gd_out = []
    for n in range(3):
        part = pl.ds(n * hrows, hrows)
        gd_out.append(pltpu.make_async_copy(
            gd_v.at[part], gd_hbm.at[0, part], out_sem.at[2 * steps + n]))
        for j in range(steps // 2):
            cols = slice(2 * j * ds, 2 * (j + 1) * ds)
            gd_v[n * hrows:(n + 1) * hrows, cols] = jnp.dot(
                hid_v[part], rg_v[:, cols], preferred_element_type=jnp.float32
            ).astype(jnp.bfloat16)
        gd_out[-1].start()

    @pl.loop(0, steps)
    def _(n):
        ggu_out(n).wait()

    for copy in layer_out + gd_out:
        copy.wait()


def finish_call(out, xlast, hidden, route_grad, grad_projected):
    cores, xs, tok, ds = out.shape
    width, seqs = xlast.shape
    half = hidden.shape[0]
    bf = jnp.bfloat16
    anyspec = pl.BlockSpec(memory_space=pl.ANY)
    return pl.pallas_call(
        finish_kernel,
        in_specs=[anyspec] * 5,
        out_specs=(anyspec,) * 3,
        out_shape=(
            jax.ShapeDtypeStruct((tok, width), bf),
            jax.ShapeDtypeStruct((1, width, 2 * half), bf),
            jax.ShapeDtypeStruct((1, half, width), bf),
        ),
        scratch_shapes=[
            pltpu.VMEM(out.shape, bf),
            pltpu.VMEM(xlast.shape, bf),
            pltpu.VMEM(hidden.shape, bf),
            pltpu.VMEM(route_grad.shape, bf),
            pltpu.VMEM(grad_projected.shape, bf),
            pltpu.VMEM((width, 2 * half), bf),
            pltpu.VMEM((half, width), bf),
            pltpu.SemaphoreType.DMA((5,)),
            pltpu.SemaphoreType.DMA((2 * NX * NC + 3,)),
        ],
        compiler_params=pltpu.CompilerParams(vmem_limit_bytes=60 * 1024 * 1024),
        name="finish",
    )(out, xlast, hidden, route_grad, grad_projected)


def body(tokens, expert_ids, gates, positives, gate_up, down):
    return finish_call(*layer_call(
        tokens, expert_ids.reshape(2, -1), gates.reshape(2, -1), positives, gate_up[0], down[0]))


def solution(mesh):
    return jax.shard_map(
        body,
        mesh=mesh,
        in_specs=(
            P("dp", None),
            P("dp", "expert"),
            P("dp", "expert"),
            P("dp"),
            P(("dp", "expert"), None, None),
            P(("dp", "expert"), None, None),
        ),
        out_specs=(P("dp", None), P(("dp", "expert"), None, None), P(("dp", "expert"), None, None)),
        check_vma=False,
    )
```

time: 121 us -> 96.3 us (0.80)
  matrix products: 9.47 us -> 0 us
  other arithmetic: 5.9 us -> 0 us
  local copies, waits for them, and re-layouts: 5.34 us -> 0 us
  Pallas kernels: 99.3 us -> 95.6 us
    dot_general x6 -> x0, matrix products: 9.47 us -> none  [the longest x1 2.63 us: body(): grad_gate_up = contract(xlast, grad_projected).astype(jnp.bfloat16)]
    pallas_call x1 -> x2, Pallas kernels: 99.3 us -> 95.6 us  [the longest x1 90.6 us: layer_call(): pl.pallas_call(layer_kernel, out_shape=(jax.ShapeDtypeStruct((NC, NX, tok...]
    convert_element_type x5 -> x0, other arithmetic: 2.44 us -> none  [the longest x1 0.68 us: body(): ml[16].astype(jnp.int32)[:, None]]
    unnamed x19 -> x0, local copies, waits for them, and re-layouts: 2.24 us -> none
    reduce_sum x3 -> x0, other arithmetic: 2.11 us -> none  [the longest x1 1.23 us: body(): norms = jnp.sqrt(jnp.sum(values * values, axis=1) + epsilon)]
    transpose x1 -> x0, local copies, waits for them, and re-layouts: 2.04 us -> none  [unslice(): return sliced.transpose(2, 1, 0, 3).reshape(seqs, cores * xs * ds)]
    concatenate x1 -> x0, other arithmetic: 1.34 us -> none  [body(): jnp.concatenate([expert_ids.astype(jnp.float32).reshape(2, 128), gates.re...]
where the time goes in v2:
time: 96.3 us; the launch traced here: 96.2 us
  Pallas kernels  95.6 us (99%)
    pallas_call x1, Pallas kernels, layer_call(): pl.pallas_call(layer_kernel, out_shape=(jax.ShapeDtypeStruct((NC, NX, tok...  90.6 us
    pallas_call x1, Pallas kernels, finish_call(): pl.pallas_call(finish_kernel, in_specs=[anyspec] * 5, out_specs=(anyspec,...  4.93 us

profile of v2, /device:TPU:1, one launch (start us, length us, event | category | flops | bytes accessed | tf_op | source)
XLA Modules:
  0.0 96.2 jit_solution(1298756293571119830)
XLA Ops:
  0.6 90.6 %layer.1 = (bf16[2,4,256,256]{3,2,1,0:T(8,128)(2,1)}, bf16[2048,128]{1,0:T(8,128)(2,1)}, bf16[384,128]{1,0:T(8,128)(2,1)}, bf16[128,2048]{1,0:T(8,128)(2,1)}, bf16[128,768]{1,0:T(8,128)(2,1)}) custom-call(bf16[256,2048]{1,0:T(8,128)(2,1)} %tok_hbm.1, s32[2,128]{1,0:T(2,128)} %bitcast.6, f32[2,128]{1,0:T(2,128)} %bitcast.7, s32[4]{0:T(128)} %pos_ref.1, ...), custom_call_target="tpu_custom_call" | custom-call | tf_op jit(solution)/shard_map/layer/pallas_call | solution.py:662
  91.3 4.9 %finish.1 = (bf16[256,2048]{1,0:T(8,128)(2,1)}, bf16[1,2048,768]{2,1,0:T(8,128)(2,1)}, bf16[1,384,2048]{2,1,0:T(8,128)(2,1)}) custom-call(bf16[2,4,256,256]{3,2,1,0:T(8,128)(2,1)} %get-tuple-element.8.out_hbm, bf16[2048,128]{1,0:T(8,128)(2,1)} %get-tuple-element.9.xlast_hbm, bf16[384,128]{1,0:T(8,128)(2,1)} %get-tuple-element.10.hid_hbm, ...), custom_call_target="tpu_custom_call" | custom-call | tf_op jit(solution)/shard_map/finish/pallas_call | solution.py:745

commit v3 on v2

--- a/solution.py
+++ b/solution.py
@@ -21,13 +21,13 @@
     tok_hbm, ids_ref, gates_ref, pos_ref, gu_hbm, dn_hbm,
     out_hbm, xlast_hbm, hid_hbm, rg_hbm, gp_hbm,
     zbuf, tokc, mb, mo, mt, rk, gw, tri, sbuf, xm, gu, dn, hid, ys, yo, yr, rs, rbuf, prec, psend, pacc, outb,
-    xly, mly, xlz, mlz, plast, kls, klo, klr, kz, kzr, ky, kx, lastz, xlast_ref, hid_ref, rg_ref, gp_ref,
+    xly, mly, xlz, mlz, plast, kls, klo, klr, kz, kzr, ky, kx, lastp, lastz, hidl, xlast_ref, hid_ref, rg_ref, gp_ref,
     loc_sem, own_sem, mb_send, mb_recv, zs_sem, zr_sem, ms_sem, mr_sem,
     xs_sem, xr_sem, xf_send, xf_recv, ys_send, ys_recv, rs_sem, rr_sem, rown_sem, ps_sem, pr_sem,
     ob_send, ob_recv, oc_send, oc_recv,
     xly_send, xly_recv, mly_send, mly_recv, xlz_send, xlz_recv, mlz_send, mlz_recv,
     xlc_send, xlc_recv, klc_send, klc_recv, kz_send, kz_recv, ky_send, ky_recv, kx_send, kx_recv,
-    lz_send, lz_recv, lc_send, lc_recv, out_sem,
+    lz_send, lz_recv, lc_send, lc_recv, ly_send, ly_recv, out_sem,
 ):
     dp = lax.axis_index("dp")
     ex = lax.axis_index("expert")
@@ -264,7 +264,7 @@
             plast[:, 2 * n * ch:2 * (n + 1) * ch] = pr
             hid[:seqs, n * ch:(n + 1) * ch] = silu_mul(pr)
         hv = hid[:seqs]
-        hid_ref[...] = hv.astype(f32).T.astype(bf)
+        hidl[...] = hv
         for xx in range(NX):
             o = jnp.dot(hv, dn[xx * NC + 1 - c], preferred_element_type=f32).astype(bf)
             kls[:, :, xx * ds:(xx + 1) * ds] = o.reshape(NZ, NY * per, ds)
@@ -314,21 +314,31 @@
         total = kx[0].astype(f32)
         for r in range(1, NX):
             total += kx[r].astype(f32)
-        lastz[c, z] = (xlz[c, z].astype(f32) + total).astype(bf)
+        last = (xlz[c, z].astype(f32) + total).astype(bf)
+        for k in range(NX):
+            lastp[k] = last[:, k * ds:(k + 1) * ds]
+        lastz[c, y, z] = lastp[y]
         for r in range(1, NZ):
-            remote(lastz.at[c, z], lastz.at[c, z], lz_send.at[r - 1], lz_recv.at[r - 1],
+            remote(lastz.at[c, y, z], lastz.at[c, y, z], lz_send.at[r - 1], lz_recv.at[r - 1],
                    z_line(r)).start()
 
+    def last_to_rows():
+        for r in range(1, NZ):
+            drain(lastp.at[0], lz_recv.at[r - 1])
+        for r in range(1, NY):
+            remote(lastz.at[c, y], lastz.at[c, y], ly_send.at[r - 1], ly_recv.at[r - 1],
+                   y_line(r)).start()
+
     def last_to_core():
-        for r in range(1, NZ):
-            drain(kz.at[0], lz_recv.at[r - 1])
+        for r in range(1, NY):
+            drain(lastz.at[0, 0], ly_recv.at[r - 1])
         remote(lastz.at[c], lastz.at[c], lc_send, lc_recv, core).start()
 
     def loss_and_rows():
         drain(lastz.at[0], lc_recv)
         dots = jnp.zeros((seqs, seqs), f32)
-        for cc in range(NC):
-            part = lastz[cc].reshape(seqs, hw)
+        for j in range(NX * NC):
+            part = lastz[j % NC, j // NC].reshape(seqs, ds)
             dots += lax.dot_general(
                 part, part, (((1,), (1,)), ((), ())), preferred_element_type=f32)
         ri = lax.broadcasted_iota(jnp.int32, (seqs, seqs), 0)
@@ -348,18 +358,14 @@
         mat = (both / (n_row * logit_divisor) - jnp.where(eye, proj / n_col, 0.0)) / n_col
         mat = mat * last_weight()
         first = mat.astype(bf)
-        rest = mat - first.astype(f32)
-        second = rest.astype(bf)
-        third = (rest - second.astype(f32)).astype(bf)
+        second = (mat - first.astype(f32)).astype(bf)
         grad_hidden = jnp.zeros((seqs, half), f32)
         for j in range(NX * NC):
-            lj = all_columns(lastz, j)
+            lj = lastz[j % NC, j // NC].reshape(seqs, ds)
             g = jnp.dot(first, lj, preferred_element_type=f32)
             g += jnp.dot(second, lj, preferred_element_type=f32)
-            g += jnp.dot(third, lj, preferred_element_type=f32)
             g = g.astype(bf)
             rg_ref[:, j * ds:(j + 1) * ds] = g
-            xlast_ref[j * ds:(j + 1) * ds, :] = all_columns(xlz, j).astype(f32).T.astype(bf)
             grad_hidden += lax.dot_general(
                 g, dn[j], (((1,), (1,)), ((), ())), preferred_element_type=f32)
         for n in range(nch):
@@ -430,11 +436,11 @@
         def _():
             swap_last_rows()
 
+    experts_last()
     send_back(5)
     send_back(4)
-    experts_last()
+    last_to_planes()
     experts(NZ // 2 - 1)
-    last_to_planes()
 
     def arrived(i):
         drain(sbuf.at[0, pl.ds(0, NQ - 1)], rr_sem.at[i])
@@ -496,14 +502,14 @@
 
         part = combine(i)
 
-        @pl.when(n < 2)
-        def _():
-            pacc[1 - n] = part
-
         @pl.when((n >= 2) & (n < 4))
         def _():
             psend[i] = part.astype(bf)
             sum_on(i)
+
+        @pl.when(n < 2)
+        def _():
+            pacc[i - 4] = part
 
         @pl.when(n == 3)
         def _():
@@ -523,18 +529,27 @@
         def _():
             drained_early()
 
+        @pl.when(n == 1)
+        def _():
+            last_to_y()
+
         @pl.when(n == 2)
         def _():
-            last_to_y()
-
-        @pl.when(n == 4)
+            hid_ref[...] = hidl[...].astype(f32).T.astype(bf)
+            for j in range(NX * NC):
+                xlast_ref[j * ds:(j + 1) * ds, :] = all_columns(xlz, j).astype(f32).T.astype(bf)
+            row_copies[0].start()
+            row_copies[1].start()
+
+        @pl.when(n == 3)
         def _():
             last_to_x()
 
-        @pl.when(n == 6)
+        @pl.when(n == 5)
         def _():
             last_to_all()
 
+    last_to_rows()
     arrived(0)
     part = combine(0)
     drain(prec.at[0], pr_sem.at[0])
@@ -569,26 +584,27 @@
             outb.at[1 - c, xx], out_hbm.at[1 - c, xx], out_sem.at[4 + r]))
         out_copies[-1].start()
 
-    take_out(0)
+    for i in range(1, NZ):
+        drain(zbuf.at[0], ps_sem.at[i])
     last_to_core()
     spread_out(1)
     spread_out(3)
+    spread_out(2)
     loss_and_rows()
-    for copy in row_copies:
+    for copy in row_copies[2:]:
         copy.start()
-    spread_out(2)
-    for r in range(1, NX):
+    for r in range(NX):
         take_out(r)
 
     for r in range(NX - 1):
         drain(outb.at[0, 0], ob_send.at[r])
     for r in range(NX):
         drain(outb.at[0, 0], oc_send.at[r])
-    for i in range(1, NZ):
-        drain(zbuf.at[0], ps_sem.at[i])
     drain(sbuf.at[0, pl.ds(0, NQ - 1)], rs_sem.at[0])
     for r in range(NZ - 1):
-        drain(kz.at[0], lz_send.at[r])
+        drain(lastp.at[0], lz_send.at[r])
+    for r in range(NY - 1):
+        drain(lastz.at[0, 0], ly_send.at[r])
     drain(lastz.at[0], lc_send)
     for copy in row_copies:
         copy.wait()
@@ -642,7 +658,9 @@
         vm((NZ, NY * per, hw), bf),
         vm((NY, NY * per, hw), bf),
         vm((NX, NY * per, hw), bf),
-        vm((NC, NZ, NY * per, hw), bf),
+        vm((NX, NY * per, ds), bf),
+        vm((NC, NY, NZ, NY * per, ds), bf),
+        vm((seqs, half), bf),
         vm((width, seqs), bf),
         vm((half, seqs), bf),
         vm((seqs, width), bf),
@@ -654,11 +672,12 @@
         dma((3,)), dma((3,)), dma((NX,)), dma((NX,)),
         dma((3,)), dma((3,)), dma((3,)), dma((3,)), dma((7,)), dma((NZ,)), dma((7,)), dma((NZ,)),
         dma, dma, dma, dma, dma((7,)), dma((7,)), dma((3,)), dma((3,)), dma((3,)), dma((3,)),
-        dma((7,)), dma((7,)), dma, dma, dma((12,)),
+        dma((7,)), dma((7,)), dma, dma, dma((3,)), dma((3,)), dma((12,)),
     ]
     anyspec = pl.BlockSpec(memory_space=pl.ANY)
     vspec = pl.BlockSpec(memory_space=pltpu.VMEM)
     sspec = pl.BlockSpec(memory_space=pltpu.SMEM)
+    hspec = pl.BlockSpec(memory_space=pltpu.HBM)
     return pl.pallas_call(
         layer_kernel,
         out_shape=(
@@ -668,11 +687,11 @@
             jax.ShapeDtypeStruct((seqs, width), bf),
             jax.ShapeDtypeStruct((seqs, 2 * half), bf),
         ),
-        in_specs=[anyspec, vspec, vspec, sspec, anyspec, anyspec],
+        in_specs=[hspec, vspec, vspec, sspec, hspec, hspec],
         out_specs=(anyspec,) * 5,
         scratch_shapes=scratch,
         compiler_params=pltpu.CompilerParams(
-            collective_id=0, has_side_effects=True, vmem_limit_bytes=60 * 1024 * 1024),
+            collective_id=0, has_side_effects=True, vmem_limit_bytes=40 * 1024 * 1024),
         name="layer",
     )(tokens, ids, gates, positives, gate_up, down)
 
@@ -762,14 +781,17 @@
             pltpu.SemaphoreType.DMA((5,)),
             pltpu.SemaphoreType.DMA((2 * NX * NC + 3,)),
         ],
-        compiler_params=pltpu.CompilerParams(vmem_limit_bytes=60 * 1024 * 1024),
+        compiler_params=pltpu.CompilerParams(vmem_limit_bytes=12 * 1024 * 1024),
         name="finish",
     )(out, xlast, hidden, route_grad, grad_projected)
 
 
 def body(tokens, expert_ids, gates, positives, gate_up, down):
+    tokens, ids, weights, weight_in, weight_out = (
+        pltpu.with_memory_space_constraint(v, pltpu.HBM) for v in (
+            tokens, expert_ids.reshape(2, -1), gates.reshape(2, -1), gate_up[0], down[0]))
     return finish_call(*layer_call(
-        tokens, expert_ids.reshape(2, -1), gates.reshape(2, -1), positives, gate_up[0], down[0]))
+        tokens, ids, weights, positives, weight_in, weight_out))
 
 
 def solution(mesh):

time: 96.3 us -> 95.6 us (level)
  Pallas kernels: 95.6 us -> 94.2 us
where the time goes in v3:
time: 95.6 us; the launch traced here: 95.5 us
  Pallas kernels  94.2 us (99%)
    pallas_call x1, Pallas kernels, layer_call(): pl.pallas_call(layer_kernel, out_shape=(jax.ShapeDtypeStruct((NC, NX, tok...  89.9 us
    pallas_call x1, Pallas kernels, finish_call(): pl.pallas_call(finish_kernel, in_specs=[anyspec] * 5, out_specs=(anyspec,...  4.29 us

profile of v3, /device:TPU:1, one launch (start us, length us, event | category | flops | bytes accessed | tf_op | source)
XLA Modules:
  0.0 95.5 jit_solution(10767648965942829566)
XLA Ops:
  0.6 0.0 copy-start
  0.6 0.6 copy-done
  1.3 89.9 %layer.1 = (bf16[2,4,256,256]{3,2,1,0:T(8,128)(2,1)S(1)}, bf16[2048,128]{1,0:T(8,128)(2,1)S(1)}, bf16[384,128]{1,0:T(8,128)(2,1)S(1)}, bf16[128,2048]{1,0:T(8,128)(2,1)S(1)}, bf16[128,768]{1,0:T(8,128)(2,1)S(1)}) custom-call(bf16[256,2048]{1,0:T(8,128)(2,1)} %tok_hbm.1, s32[2,128]{1,0:T(2,128)} %bitcast.6, f32[2,128]{1,0:T(2,128)} %bitcast.7, s32[4]{0:T(128)S(1)} %copy-done, ...), custom_call_target="tpu_custom_call" | custom-call | tf_op jit(solution)/shard_map/layer/pallas_call | solution.py:681
  91.2 4.3 %finish.1 = (bf16[256,2048]{1,0:T(8,128)(2,1)}, bf16[1,2048,768]{2,1,0:T(8,128)(2,1)}, bf16[1,384,2048]{2,1,0:T(8,128)(2,1)}) custom-call(bf16[2,4,256,256]{3,2,1,0:T(8,128)(2,1)S(1)} %get-tuple-element.8.out_hbm, bf16[2048,128]{1,0:T(8,128)(2,1)S(1)} %get-tuple-element.9.xlast_hbm, bf16[384,128]{1,0:T(8,128)(2,1)S(1)} %get-tuple-element.10.hid_hbm, ...), custom_call_target="tpu_custom_call" | custom-call | tf_op jit(solution)/shard_map/finish/pallas_call | solution.py:764
Async XLA Ops:
  0.6 0.7 copy-start
